TPU v7x, 128 devices: a whole 4x4x4 slice. The times are simulated.
128 devices in a mesh: row: 8 (over y, core), col: 16 (over x, z).
Axes of the slice: x: 4, y: 4, z: 4, core: 2. Of those that a mesh axis runs over, the one named last changes fastest.
Arguments:
- ancestor: bfloat16 [128, 128, 256, 256], P('row', 'col'), may hold values from -6 to 6
- tile_mask: int32 [128, 128], P('row', 'col'), may hold values 0 or 1
- member_one: int32 [128], replicated, may hold values 0 or 1
- member_two: int32 [128], replicated, may hold values 0 or 1
- factor_one: bfloat16 [128, 256, 256], P('row'), may hold values from -0.03125 to 0.03125
- factor_two: bfloat16 [128, 256, 256], P('row'), may hold values from -0.03125 to 0.03125
- link_block: bfloat16 [256, 256], replicated, may hold values from -0.375 to 0.375
- inverse_one: float32 [256, 256], replicated, may hold values from -6 to 6
- inverse_two: float32 [256, 256], replicated, may hold values from -6 to 6
Outputs:
- column_one: bfloat16 [128, 256, 256], P(('row', 'col'))
- column_two: bfloat16 [128, 256, 256], P(('row', 'col'))
- diag_one: bfloat16 [256, 256], replicated
- cross_block: bfloat16 [256, 256], replicated
- diag_two: bfloat16 [256, 256], replicated
All inputs are finite; a program needn't handle non-finite values. No bound on the sum of `tile_mask` on one device may be relied on, other than what follows from the above.
Results may differ from a plain program's by a relative error of at most 0.01.
Values may be sent and summed in bfloat16 or wider, within the bound.
A program may use at most 128 MiB of HBM per device.

v0:
```python
import jax
import jax.numpy as jnp
from jax import lax
from jax.sharding import PartitionSpec as P


def from_root(block, axis, owner):
    block = jnp.where(lax.axis_index(axis) == owner, block, jnp.zeros_like(block))
    return lax.psum(block, axis)


def shards(
    ancestor,
    tile_mask,
    member_one,
    member_two,
    factor_one,
    factor_two,
    link_block,
    inverse_one,
    inverse_two,
):
    hp = lax.Precision.HIGHEST
    rows_count = lax.axis_size("row")
    cols_count = lax.axis_size("col")
    row_index = lax.axis_index("row")
    col_index = lax.axis_index("col")
    rows_local = ancestor.shape[0]
    cols_local = ancestor.shape[1]
    zero = jnp.zeros((), jnp.bfloat16)
    first_start = row_index * rows_local
    flags_one = lax.dynamic_slice_in_dim(member_one, first_start, rows_local, 0)
    flags_two = lax.dynamic_slice_in_dim(member_two, first_start, rows_local, 0)
    first = jnp.where(flags_one[:, None, None] > 0, factor_one, zero)
    second = jnp.where(flags_two[:, None, None] > 0, factor_two, zero)
    group_size = cols_count // rows_count
    owner_row = col_index // group_size
    offset = col_index % group_size * cols_local
    piece_one = lax.dynamic_slice_in_dim(first, offset, cols_local, 0)
    piece_two = lax.dynamic_slice_in_dim(second, offset, cols_local, 0)
    column_first, column_second = (
        from_root(piece_one, "row", owner_row),
        from_root(piece_two, "row", owner_row),
    )
    column_both = jnp.stack([column_first, column_second], 1)
    kept = jnp.where(tile_mask[:, :, None, None] > 0, ancestor, zero)
    reduced = lax.psum_scatter(
        jnp.einsum("ijab,jkbc->ikac", kept, column_both, preferred_element_type=jnp.float32),
        "col",
        scatter_dimension=0,
        tiled=True,
    )
    own_slot = row_index * cols_count + col_index
    weight_one = lax.dynamic_slice_in_dim(member_one, own_slot, 1, 0).astype(jnp.float32)[
        :, None, None
    ]
    weight_two = lax.dynamic_slice_in_dim(member_two, own_slot, 1, 0).astype(jnp.float32)[
        :, None, None
    ]
    rows_first = lax.dynamic_slice_in_dim(first, col_index, 1, 0)
    rows_second = lax.dynamic_slice_in_dim(second, col_index, 1, 0)
    y_one = weight_one * reduced[:, 0]
    column_one = (-y_one).astype(jnp.bfloat16)
    y_two = weight_two * (
        reduced[:, 1]
        + jnp.einsum("sab,bc->sac", column_one, link_block, preferred_element_type=jnp.float32)
    )
    column_two = (-y_two).astype(jnp.bfloat16)
    v_part = jnp.einsum("sab,sac->bc", column_one, rows_second, preferred_element_type=jnp.float32)
    part_one = jnp.einsum("sab,sac->bc", rows_first.astype(jnp.float32), y_one, precision=hp)
    part_two = jnp.einsum("sab,sac->bc", rows_second.astype(jnp.float32), y_two, precision=hp)
    sum_one, vsum, carried = lax.psum((part_one, v_part, part_two), ("row", "col"))
    diag_one = (inverse_one + sum_one).astype(jnp.bfloat16)
    cross_block = (
        -(vsum + jnp.dot(diag_one, link_block, preferred_element_type=jnp.float32))
    ).astype(jnp.bfloat16)
    diag_two = (
        inverse_two
        + carried
        - jnp.dot(link_block.T, cross_block, preferred_element_type=jnp.float32)
    ).astype(jnp.bfloat16)
    return (column_one, column_two, diag_one, cross_block, diag_two)


def solution(mesh):
    in_specs = (
        P("row", "col", None, None),
        P("row", "col"),
        P(),
        P(),
        P("row", None, None),
        P("row", None, None),
        P(),
        P(),
        P(),
    )
    out_specs = (P(("row", "col"), None, None), P(("row", "col"), None, None), P(), P(), P())
    return jax.shard_map(shards, mesh=mesh, in_specs=in_specs, out_specs=out_specs, check_vma=False)
```

profile of v0, /device:TPU:1, one launch (start us, length us, event | category | flops | bytes accessed | tf_op | source)
XLA Modules:
  0.0 412.6 jit_solution(11337005895664618917)
XLA Ops:
  7.2 0.0 copy-start
  7.2 0.0 all-reduce.11.cloned.1.call-start
  7.3 3.9 copy.21
  11.2 2.9 copy.22
  14.1 0.0 copy-done.8
  14.1 0.0 copy-done.9
  14.1 0.1 dynamic-slice_compare_fusion
  14.2 1.8 broadcast_select_fusion.1
  16.0 0.0 copy-start.2
  16.0 0.2 broadcast_select_fusion
  16.2 1.1 copy-done.2
  17.3 1.2 select_bitcast_fusion.1
  18.5 0.6 copy-done.1
  19.1 1.0 select_bitcast_fusion
  20.1 0.0 all-reduce.11.cloned.1.call-update
  20.1 0.0 all-reduce.7.cloned.1.call-start
  20.2 0.0 copy-done.7
  20.2 0.1 copy.23
  20.3 67.1 %all-reduce.11.cloned.1.call-done = (bf16[8,1,256,256]{2,3,0,1:T(8,128)(2,1)}, bf16[8,1,256,256]{2,3,0,1:T(8,128)(2,1)}) async-done(((bf16[8,1,256,256]{2,3,0,1:T(8,128)(2,1)}, bf16[8,1,256,256]{2,3,0,1:T(8,128)(2,1)}), (bf16[8,1,256,256]{2,3,0,1:T(8,128)(2,1)}, bf16[8,1,256,256]{2,3,0,1:T(8,128)(2,1)})) %all-reduce.11.cloned.1.call-update) | async-done | bytes 2097168 | tf_op jit(solution)/shard_map/psum | solution.py:9
  87.4 15.1 %fusion.5 = f32[16,2,256,256]{2,3,0,1:T(8,128)} fusion(bf16[16,8,256,256]{3,2,1,0:T(8,128)(2,1)} %param.9, pred[16,8]{1,0:T(8,128)(4,1)S(1)} %copy.23, bf16[8,1,256,256]{2,3,0,1:T(8,128)(2,1)} %get-tuple-element.18, bf16[8,1,256,256]{2,3,0,1:T(8,128)(2,1)} %get-tuple-element.19), kind=kOutput, calls=%fused_computation.5 | convolution fusion | flops 8602517504 | bytes 27263104 | tf_op jit(solution)/shard_map/ijab,jkbc->ikac/dot_general | solution.py:48
  102.5 0.0 all-reduce.7.cloned.1.call-update
  102.5 0.0 all-reduce.9.cloned.1.call-start
  102.6 0.6 dynamic_slice.24
  103.1 0.6 dynamic_slice.29
  105.0 0.0 copy-done.10
  105.0 0.6 dynamic-slice
  105.6 139.7 %all-reduce.7.cloned.1.call-done = f32[16,2,256,256]{2,3,0,1:T(8,128)} async-done(((f32[16,2,256,256]{2,3,0,1:T(8,128)}), f32[16,2,256,256]{2,3,0,1:T(8,128)}) %all-reduce.7.cloned.1.call-update) | async-done | bytes 8388624
  245.3 1.7 constant_dynamic-slice_fusion
  247.1 0.1 copy.32
  247.2 0.0 copy-start.6
  247.2 1.9 fusion.20
  249.1 0.0 copy-done
  249.1 0.2 fusion.11
  249.3 0.0 copy-start.5
  249.3 2.0 fusion.18
  251.3 2.7 fusion.15
  254.0 0.0 all-reduce.9.cloned.1.call-update
  254.0 0.8 copy.26
  254.8 0.7 fusion.17
  255.5 146.4 %all-reduce.9.cloned.1.call-done = (f32[256,256]{1,0:T(8,128)}, f32[256,256]{1,0:T(8,128)}, f32[256,256]{1,0:T(8,128)}) async-done(((f32[256,256]{1,0:T(8,128)}, f32[256,256]{1,0:T(8,128)}, f32[256,256]{1,0:T(8,128)}), (f32[256,256]{1,0:T(8,128)}, f32[256,256]{1,0:T(8,128)}, f32[256,256]{1,0:T(8,128)})) %all-reduce.9.cloned.1.call-update) | async-done | bytes 786448 | tf_op jit(solution)/shard_map/psum | solution.py:72
  401.9 0.0 copy-done.6
  401.9 1.0 add_convert_fusion
  402.9 0.0 copy-start.3
  402.9 1.2 fusion.14
  404.1 0.0 copy-start.4
  404.1 0.0 copy-done.5
  404.1 1.9 fusion.13
  406.0 0.0 copy-done.3
  (7 shorter events, 0.0 us)
Async XLA Ops:
  7.2 241.9 %copy-start = (bf16[256,256]{1,0:T(8,128)(2,1)S(1)}, bf16[256,256]{1,0:T(8,128)(2,1)}, u32[]{:S(2)}) copy-start(bf16[256,256]{1,0:T(8,128)(2,1)} %param.15) | copy-start | bytes 393220
  7.2 80.2 %all-reduce.11.cloned.1.call-start = ((), (), s32[]{:S(2)}) async-start(), calls=%async_computation.2 | async-start | bytes 4194304 | tf_op jit(solution)/shard_map/psum | solution.py:9
  11.2 2.9 copy-start.8
  11.2 2.9 copy-start.9
  16.0 1.3 copy-start.2
  17.3 1.7 copy-start.1
  19.1 1.1 copy-start.7
  20.1 225.2 %all-reduce.7.cloned.1.call-start = ((), (), s32[]{:S(2)}) async-start(), calls=%async_computation | async-start | bytes 16777216
  102.5 2.6 copy-start.10
  102.5 299.4 %all-reduce.9.cloned.1.call-start = ((), (), s32[]{:S(2)}) async-start(), calls=%async_computation.1 | async-start | bytes 1572864 | tf_op jit(solution)/shard_map/psum | solution.py:72
  247.2 154.7 %copy-start.6 = (f32[256,256]{1,0:T(8,128)S(1)}, f32[256,256]{1,0:T(8,128)}, u32[]{:S(2)}) copy-start(f32[256,256]{1,0:T(8,128)} %param.16) | copy-start | bytes 786436
  249.3 154.8 %copy-start.5 = (f32[256,256]{1,0:T(8,128)S(1)}, f32[256,256]{1,0:T(8,128)}, u32[]{:S(2)}) copy-start(f32[256,256]{1,0:T(8,128)} %param.17) | copy-start | bytes 786436
  402.9 3.1 copy-start.3
  404.1 1.9 copy-start.4
Sparse Core Ops, SparseCore 0:
  20.3 67.0 all-reduce.10
  102.6 142.6 all-reduce.6
  254.2 147.7 all-reduce.8
where the time goes:
time: 413 us
  waiting for transfers between devices  353 us (85%)
  matrix products  24.9 us (6%)
  between operations  15.3 us (4%)
  local copies, waits for them, and re-layouts  11.3 us (3%)
  other arithmetic  7.64 us (2%)
    psum x1, waiting for transfers between devices, shards(): lax.psum((part_one, v_part, part_two), ('row', 'col'))  146 us
    unnamed x4, waiting for transfers between devices  140 us
    psum x1, waiting for transfers between devices, from_root(): return lax.psum(block, axis)  67.1 us
    dot_general x1, matrix products, shards(): jnp.einsum('ijab,jkbc->ikac', kept, column_both, preferred_element_type=j...  15.1 us
    unnamed x27, local copies, waits for them, and re-layouts  10 us
  transfers between devices with their start and end apart: 3, of which 3 were waited for; matrix products, arithmetic and copies ran while one was open for 1% of the time, Pallas kernels for 0%

commit v1 on v0

v1 whole, which is shorter than its diff:
```python
import jax
import jax.numpy as jnp
from jax import lax
from jax.experimental import pallas as pl
from jax.experimental.pallas import tpu as pltpu
from jax.sharding import PartitionSpec as P

MESH = pl.DeviceIdType.MESH
F32 = jnp.float32
BF16 = jnp.bfloat16
ORDER = (
    (2, 2), (2, 1), (1, 2), (2, 0), (0, 2), (2, 3), (3, 2), (1, 3),
    (3, 1), (1, 0), (0, 1), (1, 1), (3, 3), (3, 0), (0, 3), (0, 0),
)
PAIR, RING_Y, RING_X, RING_Z, BACK_X, BACK_Y, BACK_PAIR = range(7)


def pick(index, values):
    out = jnp.int32(values[0])
    for k in range(1, len(values)):
        out = jnp.where(index == k, jnp.int32(values[k]), out)
    return out


def kernel(
    anc, tm, m1, m2, f1, f2, link, inv1, inv2,
    o1, o2, od1, oc, od2,
    A, L, Fl, Pb, B1, B2, C1, C2, R, Gf, Gs, Gr1, Hb, Gr2, Ib, Gr3, Jb, Fin, lk, i1, i2,
    semA, semF, semLr, semLy, semLp, ssem, rsem, gsend, grecv,
):
    T = anc.shape[2]
    half, quarter, sub = T // 2, T // 4, T // 32
    r = lax.axis_index("row")
    c = lax.axis_index("col")
    y, core = r // 2, r % 2
    x, z = c // 4, c % 4

    def at(dx=0, dy=0, dz=0, other_core=None):
        which = core if other_core is None else other_core
        return {"row": ((y + dy) % 4) * 2 + which, "col": ((x + dx) % 4) * 4 + (z + dz) % 4}

    members = (m1, m2)

    d = (y + 4 - x) % 4
    is_src = jnp.logical_and(d == 0, core == z // 2)
    off = 8 * (z % 2)

    def local_tile(p, j):
        return pltpu.make_async_copy((f1, f2)[p].at[off + j], L.at[p, j], semLr.at[p, j])

    @pl.when(is_src)
    def _():
        for p in range(2):
            for t in range(8):
                local_tile(p, (t % 2) * 4 + t // 2).start()

    def load_row(s):
        return pltpu.make_async_copy(anc.at[s], A.at[s], semA.at[s])

    for dx, dz in ORDER:
        load_row(((x + dx) % 4) * 4 + (z + dz) % 4).start()
    small = [
        pltpu.make_async_copy(f1, Fl.at[0], semF.at[0]),
        pltpu.make_async_copy(f2, Fl.at[1], semF.at[1]),
        pltpu.make_async_copy(link, lk, semF.at[2]),
        pltpu.make_async_copy(inv1, i1, semF.at[3]),
        pltpu.make_async_copy(inv2, i2, semF.at[4]),
    ]
    for copy in small:
        copy.start()

    barrier = pltpu.get_barrier_semaphore()
    partners = [at(other_core=1 - core)]
    for o in range(1, 4):
        partners += [at(dx=o), at(dz=o), at(dy=o), at(dy=o, other_core=1 - core)]
    for partner in partners:
        pl.semaphore_signal(barrier, inc=1, device_id=partner, device_id_type=MESH)
    pl.semaphore_wait(barrier, len(partners))

    def forward_parts(p, j):
        up = j < 4
        dd = jnp.where(up, d, (4 - d) % 4)
        hub = jnp.where(up, 0, 1)
        along = pltpu.make_async_remote_copy(
            src_ref=L.at[p, j], dst_ref=L.at[p, j], send_sem=semLy.at[p, j], recv_sem=semLr.at[p, j],
            device_id=at(dy=jnp.where(up, 1, 3), other_core=hub), device_id_type=MESH,
        )
        across = pltpu.make_async_remote_copy(
            src_ref=L.at[p, j], dst_ref=L.at[p, j], send_sem=semLp.at[p, j], recv_sem=semLr.at[p, j],
            device_id=at(other_core=1 - core), device_id_type=MESH,
        )
        relay = jnp.logical_and(d != 0, core == hub)
        do_along = jnp.logical_or(is_src, jnp.logical_and(relay, dd < 3))
        do_across = jnp.logical_or(is_src, relay)
        return along, across, do_along, do_across

    def forward(p, j):
        along, across, do_along, do_across = forward_parts(p, j)

        @pl.when(is_src)
        def _():
            local_tile(p, j).wait()

        @pl.when(jnp.logical_not(is_src))
        def _():
            across.wait_recv()

        @pl.when(do_along)
        def _():
            along.start()

        @pl.when(do_across)
        def _():
            across.start()

    def forward_end(p, j):
        along, across, do_along, do_across = forward_parts(p, j)

        @pl.when(do_along)
        def _():
            along.wait_send()

        @pl.when(do_across)
        def _():
            across.wait_send()

    def slot(h, du, dv):
        dx, dz = (du, dv) if h == 0 else (dv, du)
        return ((x + dx) % 4) * 4 + (z + dz) % 4

    def rs_copy(p, h, way, m, src, dst, stage):
        step = 1 if way == 0 else 3
        device = at(dx=step) if (h == 0) == (stage == 1) else at(dz=step)
        return pltpu.make_async_remote_copy(
            src_ref=src, dst_ref=dst, send_sem=ssem.at[p, h, way, m], recv_sem=rsem.at[p, h, way, m],
            device_id=device, device_id_type=MESH,
        )

    def rows_of(h):
        return pl.ds(h * half, half)

    def first_hop(p, h, way, k, src=None):
        return rs_copy(p, h, way, k, B1.at[p, h, way, k] if src is None else src, B1.at[p, h, way, k], 1)

    def second_hop(p, h, way, dv, src=None):
        return rs_copy(p, h, way, 2 + dv, B2.at[p, h, way, dv] if src is None else src, B2.at[p, h, way, dv], 1)

    def third_hop(p, h, way):
        src = B2.at[p, h, 0, 2, pl.ds(way * quarter, quarter)]
        return rs_copy(p, h, way, 6, src, C1.at[p, h, way], 2)

    def fourth_hop(p, h, way):
        return rs_copy(p, h, way, 7, B2.at[p, h, 0, 1 if way == 0 else 3], C2.at[p, h, way], 2)

    def product(p, i):
        dx, dz = pick(i, [v[0] for v in ORDER]), pick(i, [v[1] for v in ORDER])
        s = ((x + dx) % 4) * 4 + (z + dz) % 4
        if p == 0:
            load_row(s).wait()
        own = members[p][16 * r + s]
        acc = None
        for j in range(8):
            w = (tm[s, j] * own * members[p][8 * c + j]).astype(F32)
            a = A[s, j] * jnp.full((T, T), w, F32).astype(BF16)
            term = jnp.dot(a, L[p, j], preferred_element_type=F32)
            acc = term if acc is None else acc + term
        Pb[p, s] = acc.astype(BF16)
        for h in range(2):
            du, dv = (dx, dz) if h == 0 else (dz, dx)
            inner = jnp.logical_or(dv == 1, dv == 2)
            outer = jnp.logical_not(inner)
            src = Pb.at[p, s, rows_of(h)]

            @pl.when(jnp.logical_and(du == 2, inner))
            def _():
                first_hop(p, h, 0, dv - 1, src).start()

            @pl.when(jnp.logical_and(du == 2, outer))
            def _():
                first_hop(p, h, 1, dv // 3, src).start()

            @pl.when(jnp.logical_and(du == 1, outer))
            def _():
                second_hop(p, h, 0, dv, src).start()

            @pl.when(jnp.logical_and(du == 3, inner))
            def _():
                second_hop(p, h, 1, dv, src).start()

    def add_and_pass(p):
        for k in range(2):
            for h in range(2):
                for way in range(2):
                    du, dv = (1, k + 1) if way == 0 else (3, 3 * k)
                    first_hop(p, h, way, k).wait_recv()
                    mine = Pb[p, slot(h, du, dv), rows_of(h)].astype(F32)
                    B1[p, h, way, k] = (mine + B1[p, h, way, k].astype(F32)).astype(BF16)
                    second_hop(p, h, way, dv, B1.at[p, h, way, k]).start()

    def line_sum(p, h, dv):
        for way in range(2):
            second_hop(p, h, way, dv).wait_recv()
        total = Pb[p, slot(h, 0, dv), rows_of(h)].astype(F32)
        return total + B2[p, h, 0, dv].astype(F32) + B2[p, h, 1, dv].astype(F32)

    def stage_two_far(p):
        for h in range(2):
            B2[p, h, 0, 2] = line_sum(p, h, 2).astype(BF16)
            for way in range(2):
                third_hop(p, h, way).start()

    def stage_two_near(p):
        for h in range(2):
            for way, dv in ((0, 1), (1, 3)):
                B2[p, h, 0, dv] = line_sum(p, h, dv).astype(BF16)
        for h in range(2):
            for way, dv in ((0, 1), (1, 3)):
                third_hop(p, h, way).wait_recv()
                part = pl.ds(way * quarter, quarter)
                moved = B2[p, h, 0, dv, part].astype(F32) + C1[p, h, way].astype(F32)
                B2[p, h, 0, dv, part] = moved.astype(BF16)
                fourth_hop(p, h, way).start()
        for h in range(2):
            R[p, rows_of(h)] = line_sum(p, h, 0)

    def stage_two_end(p):
        for h in range(2):
            for way in range(2):
                fourth_hop(p, h, way).wait_recv()
            R[p, rows_of(h)] = R[p, rows_of(h)] + C2[p, h, 0].astype(F32) + C2[p, h, 1].astype(F32)

    for t in range(8):
        forward(0, (t % 2) * 4 + t // 2)

    @pl.loop(0, 16)
    def _(i):
        product(0, i)

        @pl.when(i % 2 == 1)
        def _():
            t = i // 2
            forward(1, (t % 2) * 4 + t // 2)

    add_and_pass(0)

    @pl.loop(0, 16)
    def _(i):
        product(1, i)

    for copy in small:
        copy.wait()
    Gf[...] = jnp.zeros_like(Gf)

    def contract(a, b):
        return lax.dot_general(a, b, (((0,), (0,)), ((), ())), preferred_element_type=F32)

    @pl.loop(0, 16)
    def _(s):
        two = jnp.full((T, T), m2[16 * r + s].astype(F32), F32).astype(BF16)
        pieces = (
            contract(Fl[0, s], Pb[0, s]),
            contract(Fl[1, s], Pb[0, s] * two),
            contract(Fl[1, s], Pb[1, s]),
        )
        for k in range(3):
            Gf[:, k] += pieces[k].reshape(32, sub, T)

    Gs[...] = Gf[...].astype(BF16)

    def g_copy(kind, o, src, dst, device):
        return pltpu.make_async_remote_copy(
            src_ref=src, dst_ref=dst, send_sem=gsend.at[kind, o], recv_sem=grecv.at[kind, o],
            device_id=device, device_id_type=MESH,
        )

    g = core * 16 + y * 4 + x
    g_pair = g_copy(PAIR, 0, Gs.at[pl.ds((1 - core) * 16, 16)], Gr1, at(other_core=1 - core))
    g_y = [
        g_copy(RING_Y, o - 1, Hb.at[pl.ds((y + o) % 4 * 4, 4)], Gr2.at[o - 1], at(dy=o)) for o in range(1, 4)
    ]
    g_x = [g_copy(RING_X, o - 1, Ib.at[(x + o) % 4], Gr3.at[o - 1], at(dx=o)) for o in range(1, 4)]
    g_z = [g_copy(RING_Z, o - 1, Jb.at[z], Jb.at[z], at(dz=o)) for o in range(1, 4)]
    b_x = [g_copy(BACK_X, o - 1, Fin.at[g], Fin.at[g], at(dx=o)) for o in range(1, 4)]
    b_y = []
    for o in range(1, 4):
        part = Fin.at[pl.ds(core * 16 + y * 4, 4)]
        b_y.append(g_copy(BACK_Y, o - 1, part, part, at(dy=o)))
    part = Fin.at[pl.ds(core * 16, 16)]
    b_pair = g_copy(BACK_PAIR, 0, part, part, at(other_core=1 - core))

    g_pair.start()
    stage_two_far(0)
    g_pair.wait_recv()
    Hb[...] = (Gf[pl.ds(core * 16, 16)] + Gr1[...].astype(F32)).astype(BF16)
    for copy in g_y:
        copy.start()
    add_and_pass(1)
    for copy in g_y:
        copy.wait_recv()
    total = Hb[pl.ds(y * 4, 4)].astype(F32)
    for o in range(3):
        total += Gr2[o].astype(F32)
    Ib[...] = total.astype(BF16)
    for copy in g_x:
        copy.start()
    stage_two_near(0)
    for copy in g_x:
        copy.wait_recv()
    total = Ib[x].astype(F32)
    for o in range(3):
        total += Gr3[o].astype(F32)
    Jb[z] = total.astype(BF16)
    for copy in g_z:
        copy.start()
    stage_two_end(0)
    stage_two_far(1)
    for copy in g_z:
        copy.wait_recv()
    total = Jb[0].astype(F32)
    for o in range(1, 4):
        total += Jb[o].astype(F32)
    rows = pl.ds(pl.multiple_of(g * sub, sub), sub)
    Fin[g, 0] = (i1[rows] + total[0]).astype(BF16)
    Fin[g, 1] = total[1].astype(BF16)
    Fin[g, 2] = (i2[rows] + total[2]).astype(BF16)
    for copy in b_x:
        copy.start()
    stage_two_near(1)
    for copy in b_x:
        copy.wait_recv()
    for copy in b_y:
        copy.start()
    col = (-R[0]).astype(BF16)
    o1[0] = col
    linked = jnp.dot(col, lk[...], preferred_element_type=F32)
    R[0] = linked * m2[16 * r + c].astype(F32)
    for copy in b_y:
        copy.wait_recv()
    b_pair.start()
    stage_two_end(1)
    o2[0] = (-(R[1] + R[0])).astype(BF16)
    b_pair.wait_recv()
    d1 = Fin[:, 0].astype(F32).reshape(T, T).astype(BF16)
    s21 = Fin[:, 1].astype(F32).reshape(T, T)
    od1[...] = d1
    cross = (s21.T - jnp.dot(d1, lk[...], preferred_element_type=F32)).astype(BF16)
    oc[...] = cross
    d2 = Fin[:, 2].astype(F32).reshape(T, T)
    d2 = d2 - jnp.dot(s21.astype(BF16), lk[...], preferred_element_type=F32)
    od2[...] = (d2 - contract(lk[...], cross)).astype(BF16)

    for p in range(2):
        for j in range(8):
            forward_end(p, j)
        for h in range(2):
            for way in range(2):
                for k in range(2):
                    first_hop(p, h, way, k).wait_send()
                for dv in range(4):
                    second_hop(p, h, way, dv).wait_send()
                third_hop(p, h, way).wait_send()
                fourth_hop(p, h, way).wait_send()
    for copy in [g_pair, *g_y, *g_x, *g_z, *b_x, *b_y, b_pair]:
        copy.wait_send()


def shards(anc, tm, m1, m2, f1, f2, link, inv1, inv2):
    T = anc.shape[2]
    half, quarter, sub = T // 2, T // 4, T // 32
    any_space = pl.BlockSpec(memory_space=pl.ANY)
    smem = pl.BlockSpec(memory_space=pltpu.SMEM)
    vmem = pl.BlockSpec(memory_space=pltpu.VMEM)
    dma = pltpu.SemaphoreType.DMA
    tile = jax.ShapeDtypeStruct((T, T), BF16)
    column = jax.ShapeDtypeStruct((1, T, T), BF16)
    return pl.pallas_call(
        kernel,
        out_shape=(column, column, tile, tile, tile),
        in_specs=[any_space, smem, smem, smem, any_space, any_space, any_space, any_space, any_space],
        out_specs=(vmem,) * 5,
        scratch_shapes=[
            pltpu.VMEM((16, 8, T, T), BF16),
            pltpu.VMEM((2, 8, T, T), BF16),
            pltpu.VMEM((2, 16, T, T), BF16),
            pltpu.VMEM((2, 16, T, T), BF16),
            pltpu.VMEM((2, 2, 2, 2, half, T), BF16),
            pltpu.VMEM((2, 2, 2, 4, half, T), BF16),
            pltpu.VMEM((2, 2, 2, quarter, T), BF16),
            pltpu.VMEM((2, 2, 2, half, T), BF16),
            pltpu.VMEM((2, T, T), F32),
            pltpu.VMEM((32, 3, sub, T), F32),
            pltpu.VMEM((32, 3, sub, T), BF16),
            pltpu.VMEM((16, 3, sub, T), BF16),
            pltpu.VMEM((16, 3, sub, T), BF16),
            pltpu.VMEM((3, 4, 3, sub, T), BF16),
            pltpu.VMEM((4, 3, sub, T), BF16),
            pltpu.VMEM((3, 3, sub, T), BF16),
            pltpu.VMEM((4, 3, sub, T), BF16),
            pltpu.VMEM((32, 3, sub, T), BF16),
            pltpu.VMEM((T, T), BF16),
            pltpu.VMEM((T, T), F32),
            pltpu.VMEM((T, T), F32),
            dma((16,)),
            dma((5,)),
            dma((2, 8)),
            dma((2, 8)),
            dma((2, 8)),
            dma((2, 2, 2, 8)),
            dma((2, 2, 2, 8)),
            dma((7, 3)),
            dma((7, 3)),
        ],
        compiler_params=pltpu.CompilerParams(
            collective_id=0, has_side_effects=True, vmem_limit_bytes=60 * 1024 * 1024
        ),
    )(anc, tm, m1, m2, f1, f2, link, inv1, inv2)


def solution(mesh):
    in_specs = (
        P("row", "col", None, None),
        P("row", "col"),
        P(),
        P(),
        P("row", None, None),
        P("row", None, None),
        P(),
        P(),
        P(),
    )
    out_specs = (P(("row", "col"), None, None), P(("row", "col"), None, None), P(), P(), P())
    return jax.shard_map(shards, mesh=mesh, in_specs=in_specs, out_specs=out_specs, check_vma=False)
```

time: 413 us -> 207 us (0.50)
  waiting for transfers between devices: 353 us -> 0 us
  Pallas kernels: 0 us -> 196 us
  matrix products: 24.9 us -> 0 us
  between operations: 15.3 us -> 0.64 us
  other arithmetic: 7.64 us -> 0 us
    psum x2 -> x0, waiting for transfers between devices: 214 us -> none  [the longest x1 146 us: shards(): lax.psum((part_one, v_part, part_two), ('row', 'col'))]
    pallas_call x0 -> x1, Pallas kernels: none -> 196 us  [shards(): pl.pallas_call(kernel, out_shape=(column, column, tile, tile, tile), in_s...]
    unnamed x4 -> x0, waiting for transfers between devices: 140 us -> none
    dot_general x7 -> x0, matrix products: 24.9 us -> none  [the longest x1 15.1 us: shards(): jnp.einsum('ijab,jkbc->ikac', kept, column_both, preferred_element_type=j...]
    unnamed x27 -> x6, local copies, waits for them, and re-layouts: 10 us -> 9.19 us
  transfers between devices with their start and end apart: 3 -> 0, of which waited for: 3 -> 0; matrix products, arithmetic and copies ran while one was open for 1% -> 0% of each run, Pallas kernels for 0% -> 0%
where the time goes in v1:
time: 207 us; the launch traced here: 206 us
  Pallas kernels  196 us (95%)
  local copies, waits for them, and re-layouts  9.19 us (4%)
    pallas_call x1, Pallas kernels, shards(): pl.pallas_call(kernel, out_shape=(column, column, tile, tile, tile), in_s...  196 us
    unnamed x6, local copies, waits for them, and re-layouts  9.19 us

profile of v1, /device:TPU:1, one launch (start us, length us, event | category | flops | bytes accessed | tf_op | source)
XLA Modules:
  0.0 206.3 jit_solution(4625105282839251404)
XLA Ops:
  0.6 1.4 copy.14.tm
  2.0 196.5 %shard_map.128 = (bf16[1,256,256]{2,1,0:T(8,128)(2,1)}, bf16[1,256,256]{2,1,0:T(8,128)(2,1)}, bf16[256,256]{1,0:T(8,128)(2,1)}, bf16[256,256]{1,0:T(8,128)(2,1)}, bf16[256,256]{1,0:T(8,128)(2,1)}) custom-call(bf16[16,8,256,256]{3,2,1,0:T(8,128)(2,1)} %anc.1, s32[16,8]{1,0:T(8,128)} %copy.14.tm, s32[128]{0:T(128)} %m1.1, s32[128]{0:T(128)} %m2.1, ...), custom_call_target="tpu_custom_call" | custom-call | tf_op jit(solution)/shard_map/pallas_call | solution.py:376
  198.4 1.6 copy.20
  200.0 1.6 copy.21
  201.6 1.6 copy.22
  203.2 1.6 copy.23
  204.7 1.6 copy.24

commit v2 on v1

--- a/solution.py
+++ b/solution.py
@@ -77,52 +77,74 @@
         pl.semaphore_signal(barrier, inc=1, device_id=partner, device_id_type=MESH)
     pl.semaphore_wait(barrier, len(partners))
 
-    def forward_parts(p, j):
-        up = j < 4
-        dd = jnp.where(up, d, (4 - d) % 4)
-        hub = jnp.where(up, 0, 1)
-        along = pltpu.make_async_remote_copy(
+    away = jnp.where(core == 0, d, (4 - d) % 4)
+    inside = d != 0
+    relays = jnp.logical_and(inside, away < 3)
+    fed = jnp.logical_and(d == 0, jnp.logical_not(is_src))
+
+    def along(p, j, up):
+        return pltpu.make_async_remote_copy(
             src_ref=L.at[p, j], dst_ref=L.at[p, j], send_sem=semLy.at[p, j], recv_sem=semLr.at[p, j],
-            device_id=at(dy=jnp.where(up, 1, 3), other_core=hub), device_id_type=MESH,
+            device_id=at(dy=jnp.where(up, 1, 3), other_core=jnp.where(up, 0, 1)), device_id_type=MESH,
         )
-        across = pltpu.make_async_remote_copy(
+
+    def across(p, j):
+        return pltpu.make_async_remote_copy(
             src_ref=L.at[p, j], dst_ref=L.at[p, j], send_sem=semLp.at[p, j], recv_sem=semLr.at[p, j],
             device_id=at(other_core=1 - core), device_id_type=MESH,
         )
-        relay = jnp.logical_and(d != 0, core == hub)
-        do_along = jnp.logical_or(is_src, jnp.logical_and(relay, dd < 3))
-        do_across = jnp.logical_or(is_src, relay)
-        return along, across, do_along, do_across
-
-    def forward(p, j):
-        along, across, do_along, do_across = forward_parts(p, j)
+
+    def forward(p, k):
+        mine = 4 * core + k
 
         @pl.when(is_src)
         def _():
-            local_tile(p, j).wait()
-
-        @pl.when(jnp.logical_not(is_src))
-        def _():
-            across.wait_recv()
-
-        @pl.when(do_along)
-        def _():
-            along.start()
-
-        @pl.when(do_across)
-        def _():
-            across.start()
-
-    def forward_end(p, j):
-        along, across, do_along, do_across = forward_parts(p, j)
-
-        @pl.when(do_along)
-        def _():
-            along.wait_send()
-
-        @pl.when(do_across)
-        def _():
-            across.wait_send()
+            for up in (True, False):
+                j = k if up else 4 + k
+                local_tile(p, j).wait()
+                along(p, j, up).start()
+                across(p, j).start()
+
+        @pl.when(inside)
+        def _():
+            across(p, mine).wait_recv()
+
+        @pl.when(relays)
+        def _():
+            along(p, mine, core == 0).start()
+
+        @pl.when(inside)
+        def _():
+            across(p, mine).start()
+
+    def arrived(p):
+        for k in range(4):
+
+            @pl.when(jnp.logical_not(is_src))
+            def _():
+                across(p, 4 * (1 - core) + k).wait_recv()
+
+            @pl.when(fed)
+            def _():
+                across(p, 4 * core + k).wait_recv()
+
+    def forward_end(p, k):
+        mine = 4 * core + k
+
+        @pl.when(is_src)
+        def _():
+            for up in (True, False):
+                j = k if up else 4 + k
+                along(p, j, up).wait_send()
+                across(p, j).wait_send()
+
+        @pl.when(relays)
+        def _():
+            along(p, mine, core == 0).wait_send()
+
+        @pl.when(inside)
+        def _():
+            across(p, mine).wait_send()
 
     def slot(h, du, dv):
         dx, dz = (du, dv) if h == 0 else (dv, du)
@@ -160,7 +182,7 @@
         own = members[p][16 * r + s]
         acc = None
         for j in range(8):
-            w = (tm[s, j] * own * members[p][8 * c + j]).astype(F32)
+            w = (tm[j, s] * own * members[p][8 * c + j]).astype(F32)
             a = A[s, j] * jnp.full((T, T), w, F32).astype(BF16)
             term = jnp.dot(a, L[p, j], preferred_element_type=F32)
             acc = term if acc is None else acc + term
@@ -229,19 +251,20 @@
                 fourth_hop(p, h, way).wait_recv()
             R[p, rows_of(h)] = R[p, rows_of(h)] + C2[p, h, 0].astype(F32) + C2[p, h, 1].astype(F32)
 
-    for t in range(8):
-        forward(0, (t % 2) * 4 + t // 2)
+    for k in range(4):
+        forward(0, k)
+    arrived(0)
 
     @pl.loop(0, 16)
     def _(i):
         product(0, i)
 
-        @pl.when(i % 2 == 1)
-        def _():
-            t = i // 2
-            forward(1, (t % 2) * 4 + t // 2)
+        @pl.when(jnp.logical_and(i % 3 == 2, i < 12))
+        def _():
+            forward(1, i // 3)
 
     add_and_pass(0)
+    arrived(1)
 
     @pl.loop(0, 16)
     def _(i):
@@ -350,8 +373,8 @@
     od2[...] = (d2 - contract(lk[...], cross)).astype(BF16)
 
     for p in range(2):
-        for j in range(8):
-            forward_end(p, j)
+        for k in range(4):
+            forward_end(p, k)
         for h in range(2):
             for way in range(2):
                 for k in range(2):
@@ -364,6 +387,11 @@
         copy.wait_send()
 
 
+def hand_on(*refs):
+    for k in range(5):
+        refs[5 + k][...] = refs[k][...]
+
+
 def shards(anc, tm, m1, m2, f1, f2, link, inv1, inv2):
     T = anc.shape[2]
     half, quarter, sub = T // 2, T // 4, T // 32
@@ -373,7 +401,7 @@
     dma = pltpu.SemaphoreType.DMA
     tile = jax.ShapeDtypeStruct((T, T), BF16)
     column = jax.ShapeDtypeStruct((1, T, T), BF16)
-    return pl.pallas_call(
+    parts = pl.pallas_call(
         kernel,
         out_shape=(column, column, tile, tile, tile),
         in_specs=[any_space, smem, smem, smem, any_space, any_space, any_space, any_space, any_space],
@@ -413,7 +441,13 @@
         compiler_params=pltpu.CompilerParams(
             collective_id=0, has_side_effects=True, vmem_limit_bytes=60 * 1024 * 1024
         ),
-    )(anc, tm, m1, m2, f1, f2, link, inv1, inv2)
+    )(anc, tm.T, m1, m2, f1, f2, link, inv1, inv2)
+    return pl.pallas_call(
+        hand_on,
+        out_shape=(column, column, tile, tile, tile),
+        in_specs=[vmem] * 5,
+        out_specs=(vmem,) * 5,
+    )(*parts)
 
 
 def solution(mesh):

time: 207 us -> 81.9 us (0.40)
  Pallas kernels: 196 us -> 81.1 us
  local copies, waits for them, and re-layouts: 9.19 us -> 0 us
    pallas_call x1, Pallas kernels: 196 us -> 79.1 us  [shards(): pl.pallas_call(kernel, out_shape=(column, column, tile, tile, tile), in_s...]
    unnamed x6 -> x0, local copies, waits for them, and re-layouts: 9.19 us -> none
where the time goes in v2:
time: 81.9 us; the launch traced here: 81.7 us
  Pallas kernels  81.1 us (99%)
    pallas_call x1, Pallas kernels, shards(): pl.pallas_call(kernel, out_shape=(column, column, tile, tile, tile), in_s...  79.1 us
    pallas_call x1, Pallas kernels, shards(): pl.pallas_call(hand_on, out_shape=(column, column, tile, tile, tile), in_...  2 us

profile of v2, /device:TPU:1, one launch (start us, length us, event | category | flops | bytes accessed | tf_op | source)
XLA Modules:
  0.0 81.7 jit_solution(9246214918827550454)
XLA Ops:
  0.6 79.1 %shard_map.128 = (bf16[1,256,256]{2,1,0:T(8,128)(2,1)}, bf16[1,256,256]{2,1,0:T(8,128)(2,1)}, bf16[256,256]{1,0:T(8,128)(2,1)}, bf16[256,256]{1,0:T(8,128)(2,1)}, bf16[256,256]{1,0:T(8,128)(2,1)}) custom-call(bf16[16,8,256,256]{3,2,1,0:T(8,128)(2,1)} %anc.1, s32[8,16]{1,0:T(8,128)} %bitcast.1, s32[128]{0:T(128)} %m1.1, s32[128]{0:T(128)} %m2.1, ...), custom_call_target="tpu_custom_call" | custom-call | tf_op jit(solution)/shard_map/pallas_call | solution.py:404
  79.7 2.0 %shard_map.129 = (bf16[1,256,256]{2,1,0:T(8,128)(2,1)}, bf16[1,256,256]{2,1,0:T(8,128)(2,1)}, bf16[256,256]{1,0:T(8,128)(2,1)}, bf16[256,256]{1,0:T(8,128)(2,1)}, bf16[256,256]{1,0:T(8,128)(2,1)}) custom-call(bf16[1,256,256]{2,1,0:T(8,128)(2,1)} %get-tuple-element.10.refs_0_, bf16[1,256,256]{2,1,0:T(8,128)(2,1)} %get-tuple-element.11.refs_1_, ...), custom_call_target="tpu_custom_call" | custom-call | tf_op jit(solution)/shard_map/pallas_call | solution.py:445

commit v3 on v2

v3 whole, which is shorter than its diff:
```python
import jax
import jax.numpy as jnp
from jax import lax
from jax.experimental import pallas as pl
from jax.experimental.pallas import tpu as pltpu
from jax.sharding import PartitionSpec as P

MESH = pl.DeviceIdType.MESH
F32 = jnp.float32
BF16 = jnp.bfloat16
ORDER = (
    (2, 2), (2, 1), (1, 2), (2, 0), (0, 2), (2, 3), (3, 2), (1, 3),
    (3, 1), (1, 0), (0, 1), (1, 1), (3, 3), (3, 0), (0, 3), (0, 0),
)


def pick(index, values):
    out = jnp.int32(values[0])
    for k in range(1, len(values)):
        out = jnp.where(index == k, jnp.int32(values[k]), out)
    return out


def kernel(
    anc, tm, m1, m2, f1, f2, link, inv1, inv2,
    o1, o2, od1, oc, od2,
    O, semO, A, L, X, Fl, U, Pb, B1, B2, C, R, Gf, Gs, Gr1, Hb, Gr2, Jb, Fin, lk, i1, i2,
    semA, semF, semLr, semLy, semLp, semXr, semXs, semOs, ssem, rsem, gsend, grecv,
):
    T = anc.shape[2]
    half, sub = T // 2, T // 32
    r = lax.axis_index("row")
    c = lax.axis_index("col")
    y, core = r // 2, r % 2
    x, z = c // 4, c % 4

    def at(dx=0, dy=0, dz=0, other_core=None):
        which = core if other_core is None else other_core
        return {"row": ((y + dy) % 4) * 2 + which, "col": ((x + dx) % 4) * 4 + (z + dz) % 4}

    members = (m1, m2)

    d = (y + 4 - x) % 4
    own_core = core == z // 2
    off = 8 * (z % 2)
    is_src = jnp.logical_and(d == 0, own_core)
    fed = jnp.logical_and(d == 0, jnp.logical_not(own_core))
    inside = d != 0
    up_core = core == 0
    down_core = core == 1
    away = jnp.where(up_core, d, (4 - d) % 4)
    onward = (away == 1, jnp.logical_or(away == 1, away == 2))
    early = jnp.logical_or(away == 1, d == 0)

    def tile_of(k, up):
        return jnp.where(up, 0, 4) + k // 2

    def half_of(k):
        return pl.ds(k % 2 * half, half)

    def piece(p, k, up):
        return L.at[p, tile_of(k, up), half_of(k)]

    def stored(p, k, up):
        return (f1, f2)[p].at[off + tile_of(k, up), half_of(k)]

    def number(k, up):
        return jnp.where(up, 0, 8) + k

    def local_piece(p, k, up):
        return pltpu.make_async_copy(stored(p, k, up), piece(p, k, up), semLr.at[p, number(k, up)])

    def along(p, k, up, src):
        n = number(k, up)
        return pltpu.make_async_remote_copy(
            src_ref=src, dst_ref=piece(p, k, up), send_sem=semLy.at[p, n], recv_sem=semLr.at[p, n],
            device_id=at(dy=jnp.where(up, 1, 3), other_core=jnp.where(up, 0, 1)), device_id_type=MESH,
        )

    def across(p, k, up, src=None):
        n = number(k, up)
        return pltpu.make_async_remote_copy(
            src_ref=piece(p, k, up) if src is None else src, dst_ref=piece(p, k, up),
            send_sem=semLp.at[p, n], recv_sem=semLr.at[p, n],
            device_id=at(other_core=1 - core), device_id_type=MESH,
        )

    def detour_in(k, up):
        return pltpu.make_async_remote_copy(
            src_ref=stored(0, k, up), dst_ref=X.at[k], send_sem=semOs.at[k], recv_sem=semXr.at[k],
            device_id=at(dy=jnp.where(up, 3, 1), other_core=jnp.where(up, 0, 1)), device_id_type=MESH,
        )

    def detour_out(k):
        n = number(k, up_core)
        return pltpu.make_async_remote_copy(
            src_ref=X.at[k], dst_ref=piece(0, k, up_core), send_sem=semXs.at[k], recv_sem=semLr.at[0, n],
            device_id=at(dx=jnp.where(up_core, 1, 3)), device_id_type=MESH,
        )

    lends = jnp.logical_and(own_core, jnp.logical_or(d == 1, d == 3))
    lends_up = d == 1

    def load_row(s):
        return pltpu.make_async_copy(anc.at[s], A.at[s], semA.at[s])

    small = [
        pltpu.make_async_copy(f1, Fl.at[:, 0], semF.at[0]),
        pltpu.make_async_copy(f2, Fl.at[:, 1], semF.at[1]),
        pltpu.make_async_copy(link, lk, semF.at[2]),
        pltpu.make_async_copy(inv1, i1, semF.at[3]),
        pltpu.make_async_copy(inv2, i2, semF.at[4]),
    ]
    barrier = pltpu.get_barrier_semaphore()
    partners = [at(other_core=1 - core), at(dx=1), at(dx=3), at(dz=1), at(dz=3), at(dy=2)]
    for o in (1, 3):
        partners += [at(dy=o), at(dy=o, other_core=1 - core)]
    for partner in partners:
        pl.semaphore_signal(barrier, inc=1, device_id=partner, device_id_type=MESH)

    for copy in small:
        copy.start()

    @pl.when(is_src)
    def _():
        for p in range(2):

            @pl.loop(0, 8)
            def _(k):
                for up in (True, False):
                    local_piece(p, k, up).start()

    for s in range(16):
        load_row(s).start()
    pl.semaphore_wait(barrier, len(partners))

    for p in range(2):

        @pl.when(is_src)
        def _():
            @pl.loop(0, 8)
            def _(k):
                for up in (True, False):
                    along(p, k, up, stored(p, k, up)).start()

        if p == 0:

            @pl.when(lends)
            def _():
                @pl.loop(0, 8)
                def _(k):
                    detour_in(k, lends_up).start()

    @pl.when(is_src)
    def _():
        for p in range(2):

            @pl.loop(0, 8)
            def _(k):
                for up in (True, False):
                    across(p, k, up, stored(p, k, up)).start()

    for copy in small:
        copy.wait()

    @pl.loop(0, 16)
    def _(s):
        two = jnp.full((T, T), m2[16 * r + s].astype(F32), F32).astype(BF16)
        Fl[s, 0] = Fl[s, 0].T
        Fl[s, 1] = (Fl[s, 1] * two).T

    def relay(p, k):
        @pl.when(inside)
        def _():
            across(p, k, up_core).wait_recv()

            @pl.when(onward[p])
            def _():
                along(p, k, up_core, piece(p, k, up_core)).start()

            across(p, k, up_core).start()

        if p == 0:

            @pl.when(d == 0)
            def _():
                detour_in(k, up_core).wait_recv()
                detour_out(k).start()

    def arrived(p):
        @pl.loop(0, 8)
        def _(k):
            @pl.when(inside)
            def _():
                across(p, k, down_core).wait_recv()

            @pl.when(is_src)
            def _():
                for up in (True, False):
                    local_piece(p, k, up).wait()

            @pl.when(fed)
            def _():
                for up in (True, False):
                    across(p, k, up).wait_recv()

    def factors_left(p):
        @pl.loop(0, 8)
        def _(k):
            @pl.when(is_src)
            def _():
                for up in (True, False):
                    along(p, k, up, stored(p, k, up)).wait_send()
                    across(p, k, up).wait_send()

            if p == 0:

                @pl.when(lends)
                def _():
                    detour_in(k, lends_up).wait_send()

                @pl.when(d == 0)
                def _():
                    detour_out(k).wait_send()

            @pl.when(onward[p])
            def _():
                along(p, k, up_core, piece(p, k, up_core)).wait_send()

            @pl.when(inside)
            def _():
                across(p, k, up_core).wait_send()

    def slot(h, du, dv):
        dx, dz = (du, dv) if h == 0 else (dv, du)
        return ((x + dx) % 4) * 4 + (z + dz) % 4

    def rs_copy(p, h, way, m, src, dst):
        step = 1 if way == 0 else 3
        device = at(dx=step) if h == 0 else at(dz=step)
        return pltpu.make_async_remote_copy(
            src_ref=src, dst_ref=dst, send_sem=ssem.at[p, h, way, m], recv_sem=rsem.at[p, h, way, m],
            device_id=device, device_id_type=MESH,
        )

    def rows_of(h):
        return pl.ds(h * half, half)

    def first_hop(p, h, way, k, src=None):
        return rs_copy(p, h, way, k, B1.at[p, h, way, k] if src is None else src, B1.at[p, h, way, k])

    def second_hop(p, h, way, dv, src=None):
        return rs_copy(p, h, way, 2 + dv, B2.at[p, h, way, dv] if src is None else src, B2.at[p, h, way, dv])

    def third_hop(p, h, dv):
        device = at(dz=dv) if h == 0 else at(dx=dv)
        return pltpu.make_async_remote_copy(
            src_ref=B2.at[p, h, 0, dv], dst_ref=C.at[p, h, dv - 1],
            send_sem=ssem.at[p, h, 0, 5 + dv], recv_sem=rsem.at[p, h, 0, 5 + dv],
            device_id=device, device_id_type=MESH,
        )

    def product(p, pair):
        places, weights = [], []
        for e in range(2):
            i = 2 * pair + e
            dx, dz = pick(i, [v[0] for v in ORDER]), pick(i, [v[1] for v in ORDER])
            s = ((x + dx) % 4) * 4 + (z + dz) % 4
            places.append((dx, dz, s))
            weights.append(members[p][16 * r + s])
        acc = None
        for j in range(8):
            other = members[p][8 * c + j]
            a = [masked(A[s, j], tm[j, s] * own * other) for (_, _, s), own in zip(places, weights)]
            term = jnp.dot(jnp.concatenate(a, 0), L[p, j], preferred_element_type=F32)
            acc = term if acc is None else acc + term
        for e, (dx, dz, s) in enumerate(places):
            Pb[p, s] = acc[e * T : (e + 1) * T].astype(BF16)
        for dx, dz, s in places:
            send_on(p, dx, dz, s)

    def masked(a, w):
        return a * jnp.full((T, T), w.astype(F32), F32).astype(BF16)

    def send_on(p, dx, dz, s):
        for h in range(2):
            du, dv = (dx, dz) if h == 0 else (dz, dx)
            inner = jnp.logical_or(dv == 1, dv == 2)
            outer = jnp.logical_not(inner)
            src = Pb.at[p, s, rows_of(h)]

            @pl.when(jnp.logical_and(du == 2, inner))
            def _():
                first_hop(p, h, 0, dv - 1, src).start()

            @pl.when(jnp.logical_and(du == 2, outer))
            def _():
                first_hop(p, h, 1, dv // 3, src).start()

            @pl.when(jnp.logical_and(du == 1, outer))
            def _():
                second_hop(p, h, 0, dv, src).start()

            @pl.when(jnp.logical_and(du == 3, inner))
            def _():
                second_hop(p, h, 1, dv, src).start()

    def add_and_pass(p):
        for k in range(2):
            for h in range(2):
                for way in range(2):
                    du, dv = (1, k + 1) if way == 0 else (3, 3 * k)
                    first_hop(p, h, way, k).wait_recv()
                    mine = Pb[p, slot(h, du, dv), rows_of(h)].astype(F32)
                    B1[p, h, way, k] = (mine + B1[p, h, way, k].astype(F32)).astype(BF16)
                    second_hop(p, h, way, dv, B1.at[p, h, way, k]).start()

    def line_sum(p, h, dv):
        for way in range(2):
            second_hop(p, h, way, dv).wait_recv()
        total = Pb[p, slot(h, 0, dv), rows_of(h)].astype(F32)
        return total + B2[p, h, 0, dv].astype(F32) + B2[p, h, 1, dv].astype(F32)

    def stage_two(p, dv):
        for h in range(2):
            B2[p, h, 0, dv] = line_sum(p, h, dv).astype(BF16)
            third_hop(p, h, dv).start()

    def stage_two_own(p):
        for h in range(2):
            R[p, rows_of(h)] = line_sum(p, h, 0)

    def stage_two_end(p):
        for h in range(2):
            total = R[p, rows_of(h)]
            for dv in range(1, 4):
                third_hop(p, h, dv).wait_recv()
                total += C[p, h, dv - 1].astype(F32)
            R[p, rows_of(h)] = total

    def contract():
        @pl.loop(0, 4)
        def _(q):
            total = None
            for t in range(4):
                left = Fl[4 * q + t].reshape(2 * T, T)
                term = jnp.dot(left, Pb[0, 4 * q + t], preferred_element_type=F32)
                total = term if total is None else total + term
            pieces = [total[k * T : (k + 1) * T].reshape(32, sub, T) for k in range(2)]

            @pl.when(q == 0)
            def _():
                for k in range(2):
                    Gf[:, k] = pieces[k]

            @pl.when(q > 0)
            def _():
                for k in range(2):
                    Gf[:, k] += pieces[k]

    def from_left(t):
        q, j = t // 8, t % 8
        total = None
        for k in range(8):
            s = 8 * q + k
            term = jnp.dot(Fl[s, 1], masked(A[s, j], tm[j, s]), preferred_element_type=F32)
            total = term if total is None else total + term

        @pl.when(q == 0)
        def _():
            U[j] = total

        @pl.when(q > 0)
        def _():
            U[j] += total

    def finish_from_left():
        total = None
        for j in range(8):
            left = U[j].astype(BF16)
            term = jnp.dot(left, masked(L[1, j], m2[8 * c + j]), preferred_element_type=F32)
            total = term if total is None else total + term
        Gf[:, 2] = total.reshape(32, sub, T)

    @pl.loop(0, 16)
    def _(t):
        @pl.when(jnp.logical_and(early, jnp.logical_and(t >= 3, t < 11)))
        def _():
            relay(0, t - 3)

        @pl.when(jnp.logical_and(away == 1, jnp.logical_and(t >= 11, t < 15)))
        def _():
            relay(1, t - 11)

        @pl.when(jnp.logical_and(jnp.logical_not(early), t >= 8))
        def _():
            relay(0, t - 8)

        @pl.when(t % 8 == 0)
        def _():
            for k in range(8):
                load_row(t + k).wait()

        from_left(t)

    arrived(0)

    @pl.loop(0, 8)
    def _(i):
        product(0, i)

        @pl.when(away == 2)
        def _():
            relay(1, i)

        @pl.when(jnp.logical_and(away == 1, i < 4))
        def _():
            relay(1, 4 + i)

    add_and_pass(0)
    def last_hop(first):
        @pl.when(away == 3)
        def _():
            @pl.loop(first, first + 4)
            def _(k):
                relay(1, k)

    last_hop(0)
    contract()
    last_hop(4)
    arrived(1)
    finish_from_left()
    Gs[...] = Gf[...].astype(BF16)

    def out_copy(k):
        return pltpu.make_async_copy(O.at[k], (o1.at[0], o2.at[0], od1, oc, od2)[k], semO.at[k])

    def put(k, value):
        O[k] = value
        out_copy(k).start()

    def g_copy(o, src, dst, device):
        return pltpu.make_async_remote_copy(
            src_ref=src, dst_ref=dst, send_sem=gsend.at[o], recv_sem=grecv.at[o],
            device_id=device, device_id_type=MESH,
        )

    g = core * 16 + y * 4 + x
    plane = [(a, b) for a in range(4) for b in range(4) if (a, b) != (0, 0)]
    g_pair = g_copy(0, Gs.at[pl.ds((1 - core) * 16, 16)], Gr1, at(other_core=1 - core))
    b_pair = g_copy(16, Fin.at[pl.ds(core * 16, 16)], Fin.at[pl.ds(core * 16, 16)], at(other_core=1 - core))
    g_plane, b_plane = [], []
    for a, b in plane:
        n = 4 * a + b
        src = Hb.at[(y + b) % 4 * 4 + (x + a) % 4]
        g_plane.append(g_copy(n, src, Gr2.at[n], at(dx=a, dy=b)))
        b_plane.append(g_copy(16 + n, Fin.at[g], Fin.at[g], at(dx=a, dy=b)))
    g_z = [g_copy(31 + o, Jb.at[z], Jb.at[z], at(dz=o)) for o in range(1, 4)]

    g_pair.start()

    @pl.loop(0, 8)
    def _(i):
        product(1, i)

        @pl.when(i == 2)
        def _():
            stage_two(0, 2)
            g_pair.wait_recv()
            Hb[...] = (Gf[pl.ds(core * 16, 16)] + Gr1[...].astype(F32)).astype(BF16)
            for copy in g_plane:
                copy.start()

    add_and_pass(1)
    stage_two(0, 1)
    stage_two(0, 3)
    stage_two_own(0)
    for copy in g_plane:
        copy.wait_recv()
    total = Hb[y * 4 + x].astype(F32)
    for a, b in plane:
        total += Gr2[4 * a + b].astype(F32)
    Jb[z] = total.astype(BF16)
    for copy in g_z:
        copy.start()
    for copy in g_z:
        copy.wait_recv()
    total = Jb[0].astype(F32)
    for o in range(1, 4):
        total += Jb[o].astype(F32)
    rows = pl.ds(pl.multiple_of(g * sub, sub), sub)
    Fin[g, 0] = (i1[rows] + total[0]).astype(BF16)
    Fin[g, 1] = total[1].astype(BF16)
    Fin[g, 2] = (i2[rows] + total[2]).astype(BF16)
    for copy in b_plane:
        copy.start()
    stage_two_end(0)
    for dv in (2, 1, 3):
        stage_two(1, dv)
    col = (-R[0]).astype(BF16)
    put(0, col)
    R[0] = jnp.dot(col, lk[...], preferred_element_type=F32) * m2[16 * r + c].astype(F32)
    stage_two_own(1)
    for copy in b_plane:
        copy.wait_recv()
    b_pair.start()
    stage_two_end(1)
    put(1, (-(R[1] + R[0])).astype(BF16))
    b_pair.wait_recv()
    d1 = Fin[:, 0].astype(F32).reshape(T, T).astype(BF16)
    s21 = Fin[:, 1].astype(F32).reshape(T, T)
    put(2, d1)
    cross = (s21.T - jnp.dot(d1, lk[...], preferred_element_type=F32)).astype(BF16)
    put(3, cross)
    d2 = Fin[:, 2].astype(F32).reshape(T, T)
    d2 = d2 - jnp.dot(s21.astype(BF16), lk[...], preferred_element_type=F32)
    turned = lax.dot_general(lk[...], cross, (((0,), (0,)), ((), ())), preferred_element_type=F32)
    put(4, (d2 - turned).astype(BF16))

    for p in range(2):
        factors_left(p)
        for h in range(2):
            for dv in range(1, 4):
                third_hop(p, h, dv).wait_send()
            for way in range(2):
                for k in range(2):
                    first_hop(p, h, way, k).wait_send()
                for dv in range(4):
                    second_hop(p, h, way, dv).wait_send()
    for copy in [g_pair, *g_plane, *g_z, *b_plane, b_pair]:
        copy.wait_send()
    for k in range(5):
        out_copy(k).wait()


def hand_on(*refs):
    for k in range(5):
        refs[5 + k][...] = refs[k][...]


def shards(anc, tm, m1, m2, f1, f2, link, inv1, inv2):
    T = anc.shape[2]
    half, sub = T // 2, T // 32
    any_space = pl.BlockSpec(memory_space=pltpu.HBM)
    smem = pl.BlockSpec(memory_space=pltpu.SMEM)
    vmem = pl.BlockSpec(memory_space=pltpu.VMEM)
    dma = pltpu.SemaphoreType.DMA
    tile = jax.ShapeDtypeStruct((T, T), BF16)
    column = jax.ShapeDtypeStruct((1, T, T), BF16)
    parts = pl.pallas_call(
        kernel,
        out_shape=(column, column, tile, tile, tile),
        in_specs=[any_space, smem, smem, smem, any_space, any_space, any_space, any_space, any_space],
        out_specs=(any_space,) * 5,
        scratch_shapes=[
            pltpu.VMEM((5, T, T), BF16),
            dma((5,)),
            pltpu.VMEM((16, 8, T, T), BF16),
            pltpu.VMEM((2, 8, T, T), BF16),
            pltpu.VMEM((8, half, T), BF16),
            pltpu.VMEM((16, 2, T, T), BF16),
            pltpu.VMEM((8, T, T), F32),
            pltpu.VMEM((2, 16, T, T), BF16),
            pltpu.VMEM((2, 2, 2, 2, half, T), BF16),
            pltpu.VMEM((2, 2, 2, 4, half, T), BF16),
            pltpu.VMEM((2, 2, 3, half, T), BF16),
            pltpu.VMEM((2, T, T), F32),
            pltpu.VMEM((32, 3, sub, T), F32),
            pltpu.VMEM((32, 3, sub, T), BF16),
            pltpu.VMEM((16, 3, sub, T), BF16),
            pltpu.VMEM((16, 3, sub, T), BF16),
            pltpu.VMEM((16, 3, sub, T), BF16),
            pltpu.VMEM((4, 3, sub, T), BF16),
            pltpu.VMEM((32, 3, sub, T), BF16),
            pltpu.VMEM((T, T), BF16),
            pltpu.VMEM((T, T), F32),
            pltpu.VMEM((T, T), F32),
            dma((16,)),
            dma((5,)),
            dma((2, 16)),
            dma((2, 16)),
            dma((2, 16)),
            dma((8,)),
            dma((8,)),
            dma((8,)),
            dma((2, 2, 2, 9)),
            dma((2, 2, 2, 9)),
            dma((35,)),
            dma((35,)),
        ],
        compiler_params=pltpu.CompilerParams(
            collective_id=0, has_side_effects=True, vmem_limit_bytes=60 * 1024 * 1024
        ),
    )(anc, tm.T, m1, m2, f1, f2, link, inv1, inv2)
    return pl.pallas_call(
        hand_on,
        out_shape=(column, column, tile, tile, tile),
        in_specs=[vmem] * 5,
        out_specs=(vmem,) * 5,
    )(*parts)


def solution(mesh):
    in_specs = (
        P("row", "col", None, None),
        P("row", "col"),
        P(),
        P(),
        P("row", None, None),
        P("row", None, None),
        P(),
        P(),
        P(),
    )
    out_specs = (P(("row", "col"), None, None), P(("row", "col"), None, None), P(), P(), P())
    return jax.shard_map(shards, mesh=mesh, in_specs=in_specs, out_specs=out_specs, check_vma=False)
```

time: 81.9 us -> 65.9 us (0.80)
  Pallas kernels: 81.1 us -> 65.1 us
    pallas_call x1, Pallas kernels: 79.1 us -> 63.1 us  [shards(): pl.pallas_call(kernel, out_shape=(column, column, tile, tile, tile), in_s...]
where the time goes in v3:
time: 65.9 us; the launch traced here: 65.7 us
  Pallas kernels  65.1 us (99%)
    pallas_call x1, Pallas kernels, shards(): pl.pallas_call(kernel, out_shape=(column, column, tile, tile, tile), in_s...  63.1 us
    pallas_call x1, Pallas kernels, shards(): pl.pallas_call(hand_on, out_shape=(column, column, tile, tile, tile), in_...  2 us

profile of v3, /device:TPU:1, one launch (start us, length us, event | category | flops | bytes accessed | tf_op | source)
XLA Modules:
  0.0 65.7 jit_solution(2541313638223256207)
XLA Ops:
  0.6 63.1 %shard_map.128 = (bf16[1,256,256]{2,1,0:T(8,128)(2,1)}, bf16[1,256,256]{2,1,0:T(8,128)(2,1)}, bf16[256,256]{1,0:T(8,128)(2,1)}, bf16[256,256]{1,0:T(8,128)(2,1)}, bf16[256,256]{1,0:T(8,128)(2,1)}) custom-call(bf16[16,8,256,256]{3,2,1,0:T(8,128)(2,1)} %anc.1, s32[8,16]{1,0:T(8,128)} %bitcast.1, s32[128]{0:T(128)} %m1.1, s32[128]{0:T(128)} %m2.1, ...), custom_call_target="tpu_custom_call" | custom-call | tf_op jit(solution)/shard_map/pallas_call | solution.py:550
  63.7 2.0 %shard_map.129 = (bf16[1,256,256]{2,1,0:T(8,128)(2,1)}, bf16[1,256,256]{2,1,0:T(8,128)(2,1)}, bf16[256,256]{1,0:T(8,128)(2,1)}, bf16[256,256]{1,0:T(8,128)(2,1)}, bf16[256,256]{1,0:T(8,128)(2,1)}) custom-call(bf16[1,256,256]{2,1,0:T(8,128)(2,1)} %get-tuple-element.10.refs_0_, bf16[1,256,256]{2,1,0:T(8,128)(2,1)} %get-tuple-element.11.refs_1_, ...), custom_call_target="tpu_custom_call" | custom-call | tf_op jit(solution)/shard_map/pallas_call | solution.py:595

commit v4 on v3

--- a/solution.py
+++ b/solution.py
@@ -24,8 +24,8 @@
 def kernel(
     anc, tm, m1, m2, f1, f2, link, inv1, inv2,
     o1, o2, od1, oc, od2,
-    O, semO, A, L, X, Fl, U, Pb, B1, B2, C, R, Gf, Gs, Gr1, Hb, Gr2, Jb, Fin, lk, i1, i2,
-    semA, semF, semLr, semLy, semLp, semXr, semXs, semOs, ssem, rsem, gsend, grecv,
+    O, semO, A, L, X, Fl, U, Pb, B1, B2, C, R, Gf, Gs, Gr1, Hb, Gr2, Ib, Gr3, Jb, Fin, lk, i1, i2,
+    semA, semF, semLr, semLc, semLs, semXr, ssem, rsem1, rsem2, rsem3, gsend, grecv,
 ):
     T = anc.shape[2]
     half, sub = T // 2, T // 32
@@ -40,16 +40,18 @@
 
     members = (m1, m2)
 
+    def drain(ref, sem):
+        pltpu.make_async_copy(ref, ref, sem).wait()
+
+
     d = (y + 4 - x) % 4
     own_core = core == z // 2
     off = 8 * (z % 2)
     is_src = jnp.logical_and(d == 0, own_core)
-    fed = jnp.logical_and(d == 0, jnp.logical_not(own_core))
     inside = d != 0
     up_core = core == 0
     down_core = core == 1
     away = jnp.where(up_core, d, (4 - d) % 4)
-    onward = (away == 1, jnp.logical_or(away == 1, away == 2))
     early = jnp.logical_or(away == 1, d == 0)
 
     def tile_of(k, up):
@@ -64,52 +66,52 @@
     def stored(p, k, up):
         return (f1, f2)[p].at[off + tile_of(k, up), half_of(k)]
 
-    def number(k, up):
-        return jnp.where(up, 0, 8) + k
-
     def local_piece(p, k, up):
-        return pltpu.make_async_copy(stored(p, k, up), piece(p, k, up), semLr.at[p, number(k, up)])
+        return pltpu.make_async_copy(stored(p, k, up), piece(p, k, up), semLc.at[p])
 
     def along(p, k, up, src):
-        n = number(k, up)
-        return pltpu.make_async_remote_copy(
-            src_ref=src, dst_ref=piece(p, k, up), send_sem=semLy.at[p, n], recv_sem=semLr.at[p, n],
+        return pltpu.make_async_remote_copy(
+            src_ref=src, dst_ref=piece(p, k, up), send_sem=semLs.at[0], recv_sem=semLr.at[p, k],
             device_id=at(dy=jnp.where(up, 1, 3), other_core=jnp.where(up, 0, 1)), device_id_type=MESH,
         )
 
     def across(p, k, up, src=None):
-        n = number(k, up)
         return pltpu.make_async_remote_copy(
             src_ref=piece(p, k, up) if src is None else src, dst_ref=piece(p, k, up),
-            send_sem=semLp.at[p, n], recv_sem=semLr.at[p, n],
+            send_sem=semLs.at[1], recv_sem=semLc.at[p],
             device_id=at(other_core=1 - core), device_id_type=MESH,
         )
 
     def detour_in(k, up):
         return pltpu.make_async_remote_copy(
-            src_ref=stored(0, k, up), dst_ref=X.at[k], send_sem=semOs.at[k], recv_sem=semXr.at[k],
+            src_ref=stored(0, k, up), dst_ref=X.at[k], send_sem=semLs.at[2], recv_sem=semXr.at[k],
             device_id=at(dy=jnp.where(up, 3, 1), other_core=jnp.where(up, 0, 1)), device_id_type=MESH,
         )
 
     def detour_out(k):
-        n = number(k, up_core)
-        return pltpu.make_async_remote_copy(
-            src_ref=X.at[k], dst_ref=piece(0, k, up_core), send_sem=semXs.at[k], recv_sem=semLr.at[0, n],
+        return pltpu.make_async_remote_copy(
+            src_ref=X.at[k], dst_ref=piece(0, k, up_core), send_sem=semLs.at[3], recv_sem=semLr.at[0, k],
             device_id=at(dx=jnp.where(up_core, 1, 3)), device_id_type=MESH,
+        )
+
+    def straight(k, up):
+        return pltpu.make_async_remote_copy(
+            src_ref=stored(1, k, up), dst_ref=piece(1, k, up), send_sem=semLs.at[4], recv_sem=semLr.at[1, k],
+            device_id=at(dy=jnp.where(up, 3, 1), other_core=jnp.where(up, 0, 1)), device_id_type=MESH,
         )
 
     lends = jnp.logical_and(own_core, jnp.logical_or(d == 1, d == 3))
     lends_up = d == 1
 
     def load_row(s):
-        return pltpu.make_async_copy(anc.at[s], A.at[s], semA.at[s])
+        return pltpu.make_async_copy(anc.at[s], A.at[s], semA.at[s // 8])
 
     small = [
         pltpu.make_async_copy(f1, Fl.at[:, 0], semF.at[0]),
-        pltpu.make_async_copy(f2, Fl.at[:, 1], semF.at[1]),
-        pltpu.make_async_copy(link, lk, semF.at[2]),
-        pltpu.make_async_copy(inv1, i1, semF.at[3]),
-        pltpu.make_async_copy(inv2, i2, semF.at[4]),
+        pltpu.make_async_copy(f2, Fl.at[:, 1], semF.at[0]),
+        pltpu.make_async_copy(link, lk, semF.at[1]),
+        pltpu.make_async_copy(inv1, i1, semF.at[2]),
+        pltpu.make_async_copy(inv2, i2, semF.at[3]),
     ]
     barrier = pltpu.get_barrier_semaphore()
     partners = [at(other_core=1 - core), at(dx=1), at(dx=3), at(dz=1), at(dz=3), at(dy=2)]
@@ -151,6 +153,15 @@
                 def _(k):
                     detour_in(k, lends_up).start()
 
+        if p == 1:
+
+            @pl.when(is_src)
+            def _():
+                @pl.loop(0, 8)
+                def _(k):
+                    for up in (True, False):
+                        straight(k, up).start()
+
     @pl.when(is_src)
     def _():
         for p in range(2):
@@ -160,7 +171,8 @@
                 for up in (True, False):
                     across(p, k, up, stored(p, k, up)).start()
 
-    for copy in small:
+    drain(Fl, semF.at[0])
+    for copy in small[2:]:
         copy.wait()
 
     @pl.loop(0, 16)
@@ -172,9 +184,9 @@
     def relay(p, k):
         @pl.when(inside)
         def _():
-            across(p, k, up_core).wait_recv()
-
-            @pl.when(onward[p])
+            along(p, k, up_core, piece(p, k, up_core)).wait_recv()
+
+            @pl.when(away == 1)
             def _():
                 along(p, k, up_core, piece(p, k, up_core)).start()
 
@@ -188,76 +200,62 @@
                 detour_out(k).start()
 
     def arrived(p):
-        @pl.loop(0, 8)
-        def _(k):
-            @pl.when(inside)
-            def _():
-                across(p, k, down_core).wait_recv()
-
-            @pl.when(is_src)
-            def _():
-                for up in (True, False):
-                    local_piece(p, k, up).wait()
-
-            @pl.when(fed)
-            def _():
-                for up in (True, False):
-                    across(p, k, up).wait_recv()
-
-    def factors_left(p):
-        @pl.loop(0, 8)
-        def _(k):
-            @pl.when(is_src)
-            def _():
-                for up in (True, False):
-                    along(p, k, up, stored(p, k, up)).wait_send()
-                    across(p, k, up).wait_send()
-
-            if p == 0:
-
-                @pl.when(lends)
-                def _():
-                    detour_in(k, lends_up).wait_send()
-
-                @pl.when(d == 0)
-                def _():
-                    detour_out(k).wait_send()
-
-            @pl.when(onward[p])
-            def _():
-                along(p, k, up_core, piece(p, k, up_core)).wait_send()
-
-            @pl.when(inside)
-            def _():
-                across(p, k, up_core).wait_send()
+        @pl.when(inside)
+        def _():
+            drain(A.at[0, pl.ds(0, 4)], semLc.at[p])
+
+        @pl.when(d == 0)
+        def _():
+            drain(A.at[0], semLc.at[p])
+
+    def factors_left():
+        @pl.when(is_src)
+        def _():
+            drain(A.at[pl.ds(0, 2)], semLs.at[0])
+            drain(A.at[pl.ds(0, 2)], semLs.at[1])
+            drain(A.at[0], semLs.at[4])
+
+        @pl.when(away == 1)
+        def _():
+            drain(A.at[0], semLs.at[0])
+
+        @pl.when(inside)
+        def _():
+            drain(A.at[0], semLs.at[1])
+
+        @pl.when(lends)
+        def _():
+            drain(A.at[0, pl.ds(0, 4)], semLs.at[2])
+
+        @pl.when(d == 0)
+        def _():
+            drain(A.at[0, pl.ds(0, 4)], semLs.at[3])
 
     def slot(h, du, dv):
         dx, dz = (du, dv) if h == 0 else (dv, du)
         return ((x + dx) % 4) * 4 + (z + dz) % 4
 
-    def rs_copy(p, h, way, m, src, dst):
+    def rs_copy(h, way, src, dst, sem):
         step = 1 if way == 0 else 3
         device = at(dx=step) if h == 0 else at(dz=step)
         return pltpu.make_async_remote_copy(
-            src_ref=src, dst_ref=dst, send_sem=ssem.at[p, h, way, m], recv_sem=rsem.at[p, h, way, m],
-            device_id=device, device_id_type=MESH,
+            src_ref=src, dst_ref=dst, send_sem=ssem.at[0], recv_sem=sem, device_id=device, device_id_type=MESH
         )
 
     def rows_of(h):
         return pl.ds(h * half, half)
 
-    def first_hop(p, h, way, k, src=None):
-        return rs_copy(p, h, way, k, B1.at[p, h, way, k] if src is None else src, B1.at[p, h, way, k])
-
-    def second_hop(p, h, way, dv, src=None):
-        return rs_copy(p, h, way, 2 + dv, B2.at[p, h, way, dv] if src is None else src, B2.at[p, h, way, dv])
+    def first_hop(p, h, way, k, src):
+        return rs_copy(h, way, src, B1.at[p, h, way, k], rsem1.at[p, h, way])
+
+    def second_hop(p, h, way, dv, src):
+        return rs_copy(h, way, src, B2.at[p, h, dv, way], rsem2.at[p, h, dv])
 
     def third_hop(p, h, dv):
         device = at(dz=dv) if h == 0 else at(dx=dv)
         return pltpu.make_async_remote_copy(
-            src_ref=B2.at[p, h, 0, dv], dst_ref=C.at[p, h, dv - 1],
-            send_sem=ssem.at[p, h, 0, 5 + dv], recv_sem=rsem.at[p, h, 0, 5 + dv],
-            device_id=device, device_id_type=MESH,
+            src_ref=B2.at[p, h, dv, 0], dst_ref=C.at[p, h, dv - 1],
+            send_sem=ssem.at[1], recv_sem=rsem3.at[p, h], device_id=device, device_id_type=MESH,
         )
 
     def product(p, pair):
@@ -306,24 +304,23 @@
                 second_hop(p, h, 1, dv, src).start()
 
     def add_and_pass(p):
-        for k in range(2):
-            for h in range(2):
-                for way in range(2):
+        for h in range(2):
+            for way in range(2):
+                drain(B1.at[p, h, way], rsem1.at[p, h, way])
+                for k in range(2):
                     du, dv = (1, k + 1) if way == 0 else (3, 3 * k)
-                    first_hop(p, h, way, k).wait_recv()
                     mine = Pb[p, slot(h, du, dv), rows_of(h)].astype(F32)
                     B1[p, h, way, k] = (mine + B1[p, h, way, k].astype(F32)).astype(BF16)
                     second_hop(p, h, way, dv, B1.at[p, h, way, k]).start()
 
     def line_sum(p, h, dv):
-        for way in range(2):
-            second_hop(p, h, way, dv).wait_recv()
+        drain(B2.at[p, h, dv], rsem2.at[p, h, dv])
         total = Pb[p, slot(h, 0, dv), rows_of(h)].astype(F32)
-        return total + B2[p, h, 0, dv].astype(F32) + B2[p, h, 1, dv].astype(F32)
+        return total + B2[p, h, dv, 0].astype(F32) + B2[p, h, dv, 1].astype(F32)
 
     def stage_two(p, dv):
         for h in range(2):
-            B2[p, h, 0, dv] = line_sum(p, h, dv).astype(BF16)
+            B2[p, h, dv, 0] = line_sum(p, h, dv).astype(BF16)
             third_hop(p, h, dv).start()
 
     def stage_two_own(p):
@@ -333,8 +330,8 @@
     def stage_two_end(p):
         for h in range(2):
             total = R[p, rows_of(h)]
+            drain(C.at[p, h], rsem3.at[p, h])
             for dv in range(1, 4):
-                third_hop(p, h, dv).wait_recv()
                 total += C[p, h, dv - 1].astype(F32)
             R[p, rows_of(h)] = total
 
@@ -398,8 +395,7 @@
 
         @pl.when(t % 8 == 0)
         def _():
-            for k in range(8):
-                load_row(t + k).wait()
+            drain(A.at[pl.ds(0, 8)], semA.at[t // 8])
 
         from_left(t)
 
@@ -413,49 +409,50 @@
         def _():
             relay(1, i)
 
+        @pl.when(jnp.logical_and(away == 3, i >= 4))
+        def _():
+            relay(1, i - 4)
+
         @pl.when(jnp.logical_and(away == 1, i < 4))
         def _():
             relay(1, 4 + i)
 
+    contract()
+
+    @pl.when(away == 3)
+    def _():
+        @pl.loop(4, 8)
+        def _(k):
+            relay(1, k)
+
     add_and_pass(0)
-    def last_hop(first):
-        @pl.when(away == 3)
-        def _():
-            @pl.loop(first, first + 4)
-            def _(k):
-                relay(1, k)
-
-    last_hop(0)
-    contract()
-    last_hop(4)
     arrived(1)
     finish_from_left()
     Gs[...] = Gf[...].astype(BF16)
 
     def out_copy(k):
-        return pltpu.make_async_copy(O.at[k], (o1.at[0], o2.at[0], od1, oc, od2)[k], semO.at[k])
+        return pltpu.make_async_copy(O.at[k], (o1.at[0], o2.at[0], od1, oc, od2)[k], semO.at[0])
 
     def put(k, value):
         O[k] = value
         out_copy(k).start()
 
-    def g_copy(o, src, dst, device):
-        return pltpu.make_async_remote_copy(
-            src_ref=src, dst_ref=dst, send_sem=gsend.at[o], recv_sem=grecv.at[o],
+    def g_copy(kind, src, dst, device):
+        return pltpu.make_async_remote_copy(
+            src_ref=src, dst_ref=dst, send_sem=gsend.at[kind], recv_sem=grecv.at[kind],
             device_id=device, device_id_type=MESH,
         )
 
     g = core * 16 + y * 4 + x
     plane = [(a, b) for a in range(4) for b in range(4) if (a, b) != (0, 0)]
     g_pair = g_copy(0, Gs.at[pl.ds((1 - core) * 16, 16)], Gr1, at(other_core=1 - core))
-    b_pair = g_copy(16, Fin.at[pl.ds(core * 16, 16)], Fin.at[pl.ds(core * 16, 16)], at(other_core=1 - core))
-    g_plane, b_plane = [], []
+    b_pair = g_copy(5, Fin.at[pl.ds(core * 16, 16)], Fin.at[pl.ds(core * 16, 16)], at(other_core=1 - core))
+    b_plane = []
     for a, b in plane:
-        n = 4 * a + b
-        src = Hb.at[(y + b) % 4 * 4 + (x + a) % 4]
-        g_plane.append(g_copy(n, src, Gr2.at[n], at(dx=a, dy=b)))
-        b_plane.append(g_copy(16 + n, Fin.at[g], Fin.at[g], at(dx=a, dy=b)))
-    g_z = [g_copy(31 + o, Jb.at[z], Jb.at[z], at(dz=o)) for o in range(1, 4)]
+        b_plane.append(g_copy(4, Fin.at[g], Fin.at[g], at(dx=a, dy=b)))
+    g_y = [g_copy(1, Hb.at[pl.ds((y + o) % 4 * 4, 4)], Gr2.at[o - 1], at(dy=o)) for o in range(1, 4)]
+    g_x = [g_copy(2, Ib.at[(x + o) % 4], Gr3.at[o - 1], at(dx=o)) for o in range(1, 4)]
+    g_z = [g_copy(3, Jb.at[z], Jb.at[z], at(dz=o)) for o in range(1, 4)]
 
     g_pair.start()
 
@@ -463,28 +460,36 @@
     def _(i):
         product(1, i)
 
-        @pl.when(i == 2)
-        def _():
-            stage_two(0, 2)
+        @pl.when(i == 0)
+        def _():
             g_pair.wait_recv()
             Hb[...] = (Gf[pl.ds(core * 16, 16)] + Gr1[...].astype(F32)).astype(BF16)
-            for copy in g_plane:
+            for copy in g_y:
+                copy.start()
+
+        @pl.when(i == 6)
+        def _():
+            drain(Gr2, grecv.at[1])
+            total = Hb[pl.ds(y * 4, 4)].astype(F32)
+            for o in range(3):
+                total += Gr2[o].astype(F32)
+            Ib[...] = total.astype(BF16)
+            stage_two(0, 2)
+            for copy in g_x:
                 copy.start()
 
     add_and_pass(1)
     stage_two(0, 1)
     stage_two(0, 3)
     stage_two_own(0)
-    for copy in g_plane:
-        copy.wait_recv()
-    total = Hb[y * 4 + x].astype(F32)
-    for a, b in plane:
-        total += Gr2[4 * a + b].astype(F32)
+    drain(Gr3, grecv.at[2])
+    total = Ib[x].astype(F32)
+    for o in range(3):
+        total += Gr3[o].astype(F32)
     Jb[z] = total.astype(BF16)
     for copy in g_z:
         copy.start()
-    for copy in g_z:
-        copy.wait_recv()
+    drain(Jb.at[pl.ds(0, 3)], grecv.at[3])
     total = Jb[0].astype(F32)
     for o in range(1, 4):
         total += Jb[o].astype(F32)
@@ -501,8 +506,7 @@
     put(0, col)
     R[0] = jnp.dot(col, lk[...], preferred_element_type=F32) * m2[16 * r + c].astype(F32)
     stage_two_own(1)
-    for copy in b_plane:
-        copy.wait_recv()
+    drain(Fin.at[pl.ds(0, 15)], grecv.at[4])
     b_pair.start()
     stage_two_end(1)
     put(1, (-(R[1] + R[0])).astype(BF16))
@@ -517,20 +521,16 @@
     turned = lax.dot_general(lk[...], cross, (((0,), (0,)), ((), ())), preferred_element_type=F32)
     put(4, (d2 - turned).astype(BF16))
 
-    for p in range(2):
-        factors_left(p)
-        for h in range(2):
-            for dv in range(1, 4):
-                third_hop(p, h, dv).wait_send()
-            for way in range(2):
-                for k in range(2):
-                    first_hop(p, h, way, k).wait_send()
-                for dv in range(4):
-                    second_hop(p, h, way, dv).wait_send()
-    for copy in [g_pair, *g_plane, *g_z, *b_plane, b_pair]:
-        copy.wait_send()
-    for k in range(5):
-        out_copy(k).wait()
+    factors_left()
+    drain(A.at[pl.ds(0, 3)], ssem.at[0])
+    drain(A.at[0, pl.ds(0, 6)], ssem.at[1])
+    g_pair.wait_send()
+    drain(Gr2, gsend.at[1])
+    drain(Gr3, gsend.at[2])
+    drain(Jb.at[pl.ds(0, 3)], gsend.at[3])
+    drain(Fin.at[pl.ds(0, 15)], gsend.at[4])
+    b_pair.wait_send()
+    drain(O, semO.at[0])
 
 
 def hand_on(*refs):
@@ -554,7 +554,7 @@
         out_specs=(any_space,) * 5,
         scratch_shapes=[
             pltpu.VMEM((5, T, T), BF16),
-            dma((5,)),
+            dma((1,)),
             pltpu.VMEM((16, 8, T, T), BF16),
             pltpu.VMEM((2, 8, T, T), BF16),
             pltpu.VMEM((8, half, T), BF16),
@@ -562,31 +562,33 @@
             pltpu.VMEM((8, T, T), F32),
             pltpu.VMEM((2, 16, T, T), BF16),
             pltpu.VMEM((2, 2, 2, 2, half, T), BF16),
-            pltpu.VMEM((2, 2, 2, 4, half, T), BF16),
+            pltpu.VMEM((2, 2, 4, 2, half, T), BF16),
             pltpu.VMEM((2, 2, 3, half, T), BF16),
             pltpu.VMEM((2, T, T), F32),
             pltpu.VMEM((32, 3, sub, T), F32),
             pltpu.VMEM((32, 3, sub, T), BF16),
             pltpu.VMEM((16, 3, sub, T), BF16),
             pltpu.VMEM((16, 3, sub, T), BF16),
-            pltpu.VMEM((16, 3, sub, T), BF16),
+            pltpu.VMEM((3, 4, 3, sub, T), BF16),
+            pltpu.VMEM((4, 3, sub, T), BF16),
+            pltpu.VMEM((3, 3, sub, T), BF16),
             pltpu.VMEM((4, 3, sub, T), BF16),
             pltpu.VMEM((32, 3, sub, T), BF16),
             pltpu.VMEM((T, T), BF16),
             pltpu.VMEM((T, T), F32),
             pltpu.VMEM((T, T), F32),
-            dma((16,)),
+            dma((2,)),
+            dma((4,)),
+            dma((2, 8)),
+            dma((2,)),
             dma((5,)),
-            dma((2, 16)),
-            dma((2, 16)),
-            dma((2, 16)),
             dma((8,)),
-            dma((8,)),
-            dma((8,)),
-            dma((2, 2, 2, 9)),
-            dma((2, 2, 2, 9)),
-            dma((35,)),
-            dma((35,)),
+            dma((2,)),
+            dma((2, 2, 2)),
+            dma((2, 2, 4)),
+            dma((2, 2)),
+            dma((6,)),
+            dma((6,)),
         ],
         compiler_params=pltpu.CompilerParams(
             collective_id=0, has_side_effects=True, vmem_limit_bytes=60 * 1024 * 1024

time: 65.9 us -> 61.2 us (0.929)
  Pallas kernels: 65.1 us -> 60.4 us
    pallas_call x1, Pallas kernels: 63.1 us -> 58.4 us  [shards(): pl.pallas_call(kernel, out_shape=(column, column, tile, tile, tile), in_s...]
where the time goes in v4:
time: 61.2 us; the launch traced here: 61.1 us
  Pallas kernels  60.4 us (99%)
  between operations  0.64 us (1%)
    pallas_call x1, Pallas kernels, shards(): pl.pallas_call(kernel, out_shape=(column, column, tile, tile, tile), in_s...  58.4 us
    pallas_call x1, Pallas kernels, shards(): pl.pallas_call(hand_on, out_shape=(column, column, tile, tile, tile), in_...  2 us

profile of v4, /device:TPU:1, one launch (start us, length us, event | category | flops | bytes accessed | tf_op | source)
XLA Modules:
  0.0 61.1 jit_solution(8568381534801783132)
XLA Ops:
  0.6 58.4 %shard_map.128 = (bf16[1,256,256]{2,1,0:T(8,128)(2,1)}, bf16[1,256,256]{2,1,0:T(8,128)(2,1)}, bf16[256,256]{1,0:T(8,128)(2,1)}, bf16[256,256]{1,0:T(8,128)(2,1)}, bf16[256,256]{1,0:T(8,128)(2,1)}) custom-call(bf16[16,8,256,256]{3,2,1,0:T(8,128)(2,1)} %anc.1, s32[8,16]{1,0:T(8,128)} %bitcast.1, s32[128]{0:T(128)} %m1.1, s32[128]{0:T(128)} %m2.1, ...), custom_call_target="tpu_custom_call" | custom-call | tf_op jit(solution)/shard_map/pallas_call | solution.py:550
  59.1 2.0 %shard_map.129 = (bf16[1,256,256]{2,1,0:T(8,128)(2,1)}, bf16[1,256,256]{2,1,0:T(8,128)(2,1)}, bf16[256,256]{1,0:T(8,128)(2,1)}, bf16[256,256]{1,0:T(8,128)(2,1)}, bf16[256,256]{1,0:T(8,128)(2,1)}) custom-call(bf16[1,256,256]{2,1,0:T(8,128)(2,1)} %get-tuple-element.10.refs_0_, bf16[1,256,256]{2,1,0:T(8,128)(2,1)} %get-tuple-element.11.refs_1_, ...), custom_call_target="tpu_custom_call" | custom-call | tf_op jit(solution)/shard_map/pallas_call | solution.py:597

commit v5 on v4

--- a/solution.py
+++ b/solution.py
@@ -24,8 +24,8 @@
 def kernel(
     anc, tm, m1, m2, f1, f2, link, inv1, inv2,
     o1, o2, od1, oc, od2,
-    O, semO, A, L, X, Fl, U, Pb, B1, B2, C, R, Gf, Gs, Gr1, Hb, Gr2, Ib, Gr3, Jb, Fin, lk, i1, i2,
-    semA, semF, semLr, semLc, semLs, semXr, ssem, rsem1, rsem2, rsem3, gsend, grecv,
+    O, semO, A, L, X, Y, Fl, U, Pb, B1, B2, C, R, Gf, Gs, Gr1, Hb, Gr2, Ib, Gr3, Jb, Fin, lk, i1, i2,
+    semA, semF, semLr, semLc, semLs, semXr, semY, ssem, rsem0, rsem1, rsem2, rsem3, gsend, grecv,
 ):
     T = anc.shape[2]
     half, sub = T // 2, T // 32
@@ -75,16 +75,16 @@
             device_id=at(dy=jnp.where(up, 1, 3), other_core=jnp.where(up, 0, 1)), device_id_type=MESH,
         )
 
-    def across(p, k, up, src=None):
-        return pltpu.make_async_remote_copy(
-            src_ref=piece(p, k, up) if src is None else src, dst_ref=piece(p, k, up),
+    def across(p, k, up):
+        return pltpu.make_async_remote_copy(
+            src_ref=piece(p, k, up), dst_ref=piece(p, k, up),
             send_sem=semLs.at[1], recv_sem=semLc.at[p],
             device_id=at(other_core=1 - core), device_id_type=MESH,
         )
 
     def detour_in(k, up):
         return pltpu.make_async_remote_copy(
-            src_ref=stored(0, k, up), dst_ref=X.at[k], send_sem=semLs.at[2], recv_sem=semXr.at[k],
+            src_ref=Y.at[k], dst_ref=X.at[k], send_sem=semLs.at[2], recv_sem=semXr.at[k],
             device_id=at(dy=jnp.where(up, 3, 1), other_core=jnp.where(up, 0, 1)), device_id_type=MESH,
         )
 
@@ -96,7 +96,7 @@
 
     def straight(k, up):
         return pltpu.make_async_remote_copy(
-            src_ref=stored(1, k, up), dst_ref=piece(1, k, up), send_sem=semLs.at[4], recv_sem=semLr.at[1, k],
+            src_ref=piece(1, k, up), dst_ref=piece(1, k, up), send_sem=semLs.at[4], recv_sem=semLr.at[1, k],
             device_id=at(dy=jnp.where(up, 3, 1), other_core=jnp.where(up, 0, 1)), device_id_type=MESH,
         )
 
@@ -114,24 +114,34 @@
         pltpu.make_async_copy(inv2, i2, semF.at[3]),
     ]
     barrier = pltpu.get_barrier_semaphore()
-    partners = [at(other_core=1 - core), at(dx=1), at(dx=3), at(dz=1), at(dz=3), at(dy=2)]
+    partners = [at(other_core=1 - core), at(dx=1), at(dx=3), at(dz=1), at(dz=3), at(dx=2), at(dy=2), at(dz=2)]
     for o in (1, 3):
         partners += [at(dy=o), at(dy=o, other_core=1 - core)]
     for partner in partners:
         pl.semaphore_signal(barrier, inc=1, device_id=partner, device_id_type=MESH)
 
-    for copy in small:
-        copy.start()
-
-    @pl.when(is_src)
+    def lent(k):
+        return pltpu.make_async_copy(stored(0, k, lends_up), Y.at[k], semY.at[0])
+
+    @pl.when(lends)
     def _():
-        for p in range(2):
-
+        @pl.loop(0, 8)
+        def _(k):
+            lent(k).start()
+
+    for p in range(2):
+
+        @pl.when(is_src)
+        def _():
             @pl.loop(0, 8)
             def _(k):
                 for up in (True, False):
                     local_piece(p, k, up).start()
 
+        if p == 0:
+            for copy in small:
+                copy.start()
+
     for s in range(16):
         load_row(s).start()
     pl.semaphore_wait(barrier, len(partners))
@@ -140,15 +150,19 @@
 
         @pl.when(is_src)
         def _():
+            drain(A.at[0], semLc.at[p])
+
             @pl.loop(0, 8)
             def _(k):
                 for up in (True, False):
-                    along(p, k, up, stored(p, k, up)).start()
+                    along(p, k, up, piece(p, k, up)).start()
 
         if p == 0:
 
             @pl.when(lends)
             def _():
+                drain(A.at[0, pl.ds(0, 4)], semY.at[0])
+
                 @pl.loop(0, 8)
                 def _(k):
                     detour_in(k, lends_up).start()
@@ -169,7 +183,7 @@
             @pl.loop(0, 8)
             def _(k):
                 for up in (True, False):
-                    across(p, k, up, stored(p, k, up)).start()
+                    across(p, k, up).start()
 
     drain(Fl, semF.at[0])
     for copy in small[2:]:
@@ -204,7 +218,7 @@
         def _():
             drain(A.at[0, pl.ds(0, 4)], semLc.at[p])
 
-        @pl.when(d == 0)
+        @pl.when(jnp.logical_and(d == 0, jnp.logical_not(own_core)))
         def _():
             drain(A.at[0], semLc.at[p])
 
@@ -250,6 +264,13 @@
 
     def second_hop(p, h, way, dv, src):
         return rs_copy(h, way, src, B2.at[p, h, dv, way], rsem2.at[p, h, dv])
+
+    def two_away(h, dv, src):
+        device = at(dx=2) if h == 0 else at(dz=2)
+        return pltpu.make_async_remote_copy(
+            src_ref=src, dst_ref=B1.at[0, h, dv // 2, dv % 2],
+            send_sem=ssem.at[0], recv_sem=rsem0.at[h, dv], device_id=device, device_id_type=MESH,
+        )
 
     def third_hop(p, h, dv):
         device = at(dz=dv) if h == 0 else at(dx=dv)
@@ -287,6 +308,22 @@
             outer = jnp.logical_not(inner)
             src = Pb.at[p, s, rows_of(h)]
 
+            if p == 0:
+
+                @pl.when(du == 1)
+                def _():
+                    second_hop(0, h, 0, dv, src).start()
+
+                @pl.when(du == 3)
+                def _():
+                    second_hop(0, h, 1, dv, src).start()
+
+                @pl.when(du == 2)
+                def _():
+                    two_away(h, dv, src).start()
+
+                continue
+
             @pl.when(jnp.logical_and(du == 2, inner))
             def _():
                 first_hop(p, h, 0, dv - 1, src).start()
@@ -307,7 +344,7 @@
         for h in range(2):
             for way in range(2):
                 drain(B1.at[p, h, way], rsem1.at[p, h, way])
-                for k in range(2):
+                for k in (1, 0):
                     du, dv = (1, k + 1) if way == 0 else (3, 3 * k)
                     mine = Pb[p, slot(h, du, dv), rows_of(h)].astype(F32)
                     B1[p, h, way, k] = (mine + B1[p, h, way, k].astype(F32)).astype(BF16)
@@ -316,11 +353,19 @@
     def line_sum(p, h, dv):
         drain(B2.at[p, h, dv], rsem2.at[p, h, dv])
         total = Pb[p, slot(h, 0, dv), rows_of(h)].astype(F32)
-        return total + B2[p, h, dv, 0].astype(F32) + B2[p, h, dv, 1].astype(F32)
-
-    def stage_two(p, dv):
+        total += B2[p, h, dv, 0].astype(F32) + B2[p, h, dv, 1].astype(F32)
+        if p == 0:
+            drain(B1.at[0, h, dv // 2, dv % 2], rsem0.at[h, dv])
+            total += B1[0, h, dv // 2, dv % 2].astype(F32)
+        return total
+
+    def stage_two_sum(p, dv):
         for h in range(2):
             B2[p, h, dv, 0] = line_sum(p, h, dv).astype(BF16)
+
+    def stage_two(p, dv):
+        stage_two_sum(p, dv)
+        for h in range(2):
             third_hop(p, h, dv).start()
 
     def stage_two_own(p):
@@ -425,7 +470,6 @@
         def _(k):
             relay(1, k)
 
-    add_and_pass(0)
     arrived(1)
     finish_from_left()
     Gs[...] = Gf[...].astype(BF16)
@@ -445,14 +489,15 @@
 
     g = core * 16 + y * 4 + x
     plane = [(a, b) for a in range(4) for b in range(4) if (a, b) != (0, 0)]
+    plane.sort(key=lambda v: -sum(min(e, 4 - e) for e in v))
     g_pair = g_copy(0, Gs.at[pl.ds((1 - core) * 16, 16)], Gr1, at(other_core=1 - core))
     b_pair = g_copy(5, Fin.at[pl.ds(core * 16, 16)], Fin.at[pl.ds(core * 16, 16)], at(other_core=1 - core))
     b_plane = []
     for a, b in plane:
         b_plane.append(g_copy(4, Fin.at[g], Fin.at[g], at(dx=a, dy=b)))
-    g_y = [g_copy(1, Hb.at[pl.ds((y + o) % 4 * 4, 4)], Gr2.at[o - 1], at(dy=o)) for o in range(1, 4)]
-    g_x = [g_copy(2, Ib.at[(x + o) % 4], Gr3.at[o - 1], at(dx=o)) for o in range(1, 4)]
-    g_z = [g_copy(3, Jb.at[z], Jb.at[z], at(dz=o)) for o in range(1, 4)]
+    g_y = [g_copy(1, Hb.at[pl.ds((y + o) % 4 * 4, 4)], Gr2.at[o - 1], at(dy=o)) for o in (2, 1, 3)]
+    g_x = [g_copy(2, Ib.at[(x + o) % 4], Gr3.at[o - 1], at(dx=o)) for o in (2, 1, 3)]
+    g_z = [g_copy(3, Jb.at[z], Jb.at[z], at(dz=o)) for o in (2, 1, 3)]
 
     g_pair.start()
 
@@ -474,14 +519,13 @@
             for o in range(3):
                 total += Gr2[o].astype(F32)
             Ib[...] = total.astype(BF16)
-            stage_two(0, 2)
+            stage_two_sum(0, 2)
             for copy in g_x:
                 copy.start()
+            for h in range(2):
+                third_hop(0, h, 2).start()
 
     add_and_pass(1)
-    stage_two(0, 1)
-    stage_two(0, 3)
-    stage_two_own(0)
     drain(Gr3, grecv.at[2])
     total = Ib[x].astype(F32)
     for o in range(3):
@@ -489,6 +533,10 @@
     Jb[z] = total.astype(BF16)
     for copy in g_z:
         copy.start()
+    stage_two(0, 1)
+    stage_two(0, 3)
+    stage_two_own(0)
+    stage_two(1, 2)
     drain(Jb.at[pl.ds(0, 3)], grecv.at[3])
     total = Jb[0].astype(F32)
     for o in range(1, 4):
@@ -499,13 +547,13 @@
     Fin[g, 2] = (i2[rows] + total[2]).astype(BF16)
     for copy in b_plane:
         copy.start()
+    for dv in (1, 3):
+        stage_two(1, dv)
+    stage_two_own(1)
     stage_two_end(0)
-    for dv in (2, 1, 3):
-        stage_two(1, dv)
     col = (-R[0]).astype(BF16)
     put(0, col)
     R[0] = jnp.dot(col, lk[...], preferred_element_type=F32) * m2[16 * r + c].astype(F32)
-    stage_two_own(1)
     drain(Fin.at[pl.ds(0, 15)], grecv.at[4])
     b_pair.start()
     stage_two_end(1)
@@ -557,6 +605,7 @@
             dma((1,)),
             pltpu.VMEM((16, 8, T, T), BF16),
             pltpu.VMEM((2, 8, T, T), BF16),
+            pltpu.VMEM((8, half, T), BF16),
             pltpu.VMEM((8, half, T), BF16),
             pltpu.VMEM((16, 2, T, T), BF16),
             pltpu.VMEM((8, T, T), F32),
@@ -583,7 +632,9 @@
             dma((2,)),
             dma((5,)),
             dma((8,)),
+            dma((1,)),
             dma((2,)),
+            dma((2, 4)),
             dma((2, 2, 2)),
             dma((2, 2, 4)),
             dma((2, 2)),

time: 61.2 us -> 59.7 us (0.975)
  Pallas kernels: 60.4 us -> 58.9 us
    pallas_call x1, Pallas kernels: 58.4 us -> 56.9 us  [shards(): pl.pallas_call(kernel, out_shape=(column, column, tile, tile, tile), in_s...]
where the time goes in v5:
time: 59.7 us; the launch traced here: 59.6 us
  Pallas kernels  58.9 us (99%)
  between operations  0.64 us (1%)
    pallas_call x1, Pallas kernels, shards(): pl.pallas_call(kernel, out_shape=(column, column, tile, tile, tile), in_s...  56.9 us
    pallas_call x1, Pallas kernels, shards(): pl.pallas_call(hand_on, out_shape=(column, column, tile, tile, tile), in_...  2 us

profile of v5, /device:TPU:1, one launch (start us, length us, event | category | flops | bytes accessed | tf_op | source)
XLA Modules:
  0.0 59.6 jit_solution(1749150165619334631)
XLA Ops:
  0.6 56.9 %shard_map.128 = (bf16[1,256,256]{2,1,0:T(8,128)(2,1)}, bf16[1,256,256]{2,1,0:T(8,128)(2,1)}, bf16[256,256]{1,0:T(8,128)(2,1)}, bf16[256,256]{1,0:T(8,128)(2,1)}, bf16[256,256]{1,0:T(8,128)(2,1)}) custom-call(bf16[16,8,256,256]{3,2,1,0:T(8,128)(2,1)} %anc.1, s32[8,16]{1,0:T(8,128)} %bitcast.1, s32[128]{0:T(128)} %m1.1, s32[128]{0:T(128)} %m2.1, ...), custom_call_target="tpu_custom_call" | custom-call | tf_op jit(solution)/shard_map/pallas_call | solution.py:598
  57.6 2.0 %shard_map.129 = (bf16[1,256,256]{2,1,0:T(8,128)(2,1)}, bf16[1,256,256]{2,1,0:T(8,128)(2,1)}, bf16[256,256]{1,0:T(8,128)(2,1)}, bf16[256,256]{1,0:T(8,128)(2,1)}, bf16[256,256]{1,0:T(8,128)(2,1)}) custom-call(bf16[1,256,256]{2,1,0:T(8,128)(2,1)} %get-tuple-element.10.refs_0_, bf16[1,256,256]{2,1,0:T(8,128)(2,1)} %get-tuple-element.11.refs_1_, ...), custom_call_target="tpu_custom_call" | custom-call | tf_op jit(solution)/shard_map/pallas_call | solution.py:648

commit v6 on v5

--- a/solution.py
+++ b/solution.py
@@ -22,9 +22,9 @@
 
 
 def kernel(
-    anc, tm, m1, m2, f1, f2, link, inv1, inv2,
+    anc, tm_in, m1_in, m2_in, f1, f2, link, inv1, inv2,
     o1, o2, od1, oc, od2,
-    O, semO, A, L, X, Y, Fl, U, Pb, B1, B2, C, R, Gf, Gs, Gr1, Hb, Gr2, Ib, Gr3, Jb, Fin, lk, i1, i2,
+    O, semO, tm, m1, m2, A, L, X, Y, Fl, U, Pb, B1, B2, C, R, Gf, Gs, Gr1, Hb, Gr2, Ib, Gr3, Jb, Fin, lk, i1, i2,
     semA, semF, semLr, semLc, semLs, semXr, semY, ssem, rsem0, rsem1, rsem2, rsem3, gsend, grecv,
 ):
     T = anc.shape[2]
@@ -112,6 +112,9 @@
         pltpu.make_async_copy(link, lk, semF.at[1]),
         pltpu.make_async_copy(inv1, i1, semF.at[2]),
         pltpu.make_async_copy(inv2, i2, semF.at[3]),
+        pltpu.make_async_copy(tm_in, tm, semF.at[4]),
+        pltpu.make_async_copy(m1_in, m1, semF.at[5]),
+        pltpu.make_async_copy(m2_in, m2, semF.at[6]),
     ]
     barrier = pltpu.get_barrier_semaphore()
     partners = [at(other_core=1 - core), at(dx=1), at(dx=3), at(dz=1), at(dz=3), at(dx=2), at(dy=2), at(dz=2)]
@@ -590,7 +593,6 @@
     T = anc.shape[2]
     half, sub = T // 2, T // 32
     any_space = pl.BlockSpec(memory_space=pltpu.HBM)
-    smem = pl.BlockSpec(memory_space=pltpu.SMEM)
     vmem = pl.BlockSpec(memory_space=pltpu.VMEM)
     dma = pltpu.SemaphoreType.DMA
     tile = jax.ShapeDtypeStruct((T, T), BF16)
@@ -598,11 +600,14 @@
     parts = pl.pallas_call(
         kernel,
         out_shape=(column, column, tile, tile, tile),
-        in_specs=[any_space, smem, smem, smem, any_space, any_space, any_space, any_space, any_space],
+        in_specs=[any_space, any_space, any_space, any_space, any_space, any_space, any_space, any_space, any_space],
         out_specs=(any_space,) * 5,
         scratch_shapes=[
             pltpu.VMEM((5, T, T), BF16),
             dma((1,)),
+            pltpu.SMEM(tm.shape[::-1], jnp.int32),
+            pltpu.SMEM(m1.shape, jnp.int32),
+            pltpu.SMEM(m2.shape, jnp.int32),
             pltpu.VMEM((16, 8, T, T), BF16),
             pltpu.VMEM((2, 8, T, T), BF16),
             pltpu.VMEM((8, half, T), BF16),
@@ -627,7 +632,7 @@
             pltpu.VMEM((T, T), F32),
             pltpu.VMEM((T, T), F32),
             dma((2,)),
-            dma((4,)),
+            dma((7,)),
             dma((2, 8)),
             dma((2,)),
             dma((5,)),

time: 59.7 us -> 59 us (0.988)
  Pallas kernels: 58.9 us -> 58.2 us
    pallas_call x1, Pallas kernels: 56.9 us -> 56.2 us  [shards(): pl.pallas_call(kernel, out_shape=(column, column, tile, tile, tile), in_s...]
where the time goes in v6:
time: 59 us; the launch traced here: 58.9 us
  Pallas kernels  58.2 us (99%)
  between operations  0.64 us (1%)
    pallas_call x1, Pallas kernels, shards(): pl.pallas_call(kernel, out_shape=(column, column, tile, tile, tile), in_s...  56.2 us
    pallas_call x1, Pallas kernels, shards(): pl.pallas_call(hand_on, out_shape=(column, column, tile, tile, tile), in_...  2 us

profile of v6, /device:TPU:1, one launch (start us, length us, event | category | flops | bytes accessed | tf_op | source)
XLA Modules:
  0.0 58.9 jit_solution(5621977874100715322)
XLA Ops:
  0.6 56.2 %shard_map.128 = (bf16[1,256,256]{2,1,0:T(8,128)(2,1)}, bf16[1,256,256]{2,1,0:T(8,128)(2,1)}, bf16[256,256]{1,0:T(8,128)(2,1)}, bf16[256,256]{1,0:T(8,128)(2,1)}, bf16[256,256]{1,0:T(8,128)(2,1)}) custom-call(bf16[16,8,256,256]{3,2,1,0:T(8,128)(2,1)} %anc.1, s32[8,16]{1,0:T(8,128)} %bitcast.1, s32[128]{0:T(128)} %m1_in.1, s32[128]{0:T(128)} %m2_in.1, ...), custom_call_target="tpu_custom_call" | custom-call | tf_op jit(solution)/shard_map/pallas_call | solution.py:600
  56.8 2.0 %shard_map.129 = (bf16[1,256,256]{2,1,0:T(8,128)(2,1)}, bf16[1,256,256]{2,1,0:T(8,128)(2,1)}, bf16[256,256]{1,0:T(8,128)(2,1)}, bf16[256,256]{1,0:T(8,128)(2,1)}, bf16[256,256]{1,0:T(8,128)(2,1)}) custom-call(bf16[1,256,256]{2,1,0:T(8,128)(2,1)} %get-tuple-element.10.refs_0_, bf16[1,256,256]{2,1,0:T(8,128)(2,1)} %get-tuple-element.11.refs_1_, ...), custom_call_target="tpu_custom_call" | custom-call | tf_op jit(solution)/shard_map/pallas_call | solution.py:653
